TPU v7x, 512 devices: a whole 4x8x8 slice. The times are simulated.
512 devices in a mesh: dp: 16 (over z, core), space: 32 (over x, y).
Axes of the slice: x: 4, y: 8, z: 8, core: 2. Of those that a mesh axis runs over, the one named last changes fastest.
Arguments:
- features: bfloat16 [16, 32, 128, 32, 128], P('dp', None, 'space'), may hold values from -6 to 6
- cotangent: bfloat16 [16, 32, 128, 32, 128], P('dp', None, 'space'), may hold values from -6 to 6
- spectral: bfloat16 [256, 32, 2048], P('space', 'dp'), may hold values from -3 to 3
- pointwise: bfloat16 [32, 32], replicated, may hold values from -1 to 1
- biases: bfloat16 [32], replicated, may hold values from -3 to 3
Outputs:
- grad_input: bfloat16 [16, 32, 128, 32, 128], P('dp', None, 'space')
- grad_spectral: float32 [256, 32, 2048], P('space', 'dp')
All inputs are finite; a program needn't handle non-finite values.
Results may differ from a plain program's by a relative error of at most 0.025.
Values may be sent and summed in bfloat16 or wider, within the bound.
No kernel may reach another device: no remote copies, remote signals or barrier semaphores. Data moves between devices by JAX's collectives and lax.ppermute only.
A program may use at most 64 MiB of HBM per device.

v0:
```python
import math

import jax
import jax.numpy as jnp
from jax import lax
from jax.sharding import PartitionSpec as P

KX = 32
KY = 32
KZ = 8


tanh_coef = 0.7978845608028654
cubic_coef = 0.044715


def frequencies(kept_count, length):
    indices = jnp.arange(kept_count, dtype=jnp.int32)
    return jnp.where(indices < kept_count // 2, indices, indices + (length - kept_count))


def plane_table(count_y, count_z, kept_y, kept_z):
    freq_y = frequencies(kept_y, count_y)
    freq_z = jnp.arange(kept_z, dtype=jnp.int32)
    turn_y = jnp.arange(count_y, dtype=jnp.int32)[:, None] * freq_y[None, :] % count_y
    turn_z = jnp.arange(count_z, dtype=jnp.int32)[:, None] * freq_z[None, :] % count_z
    angles = (
        2.0
        * math.pi
        * (
            turn_y[:, None, :, None].astype(jnp.float32) / count_y
            + turn_z[None, :, None, :].astype(jnp.float32) / count_z
        )
    )
    factor = 1.0 / math.sqrt(count_y * count_z)
    basis_table = jnp.stack([factor * jnp.cos(angles), -factor * jnp.sin(angles)], axis=-1)
    return basis_table.reshape(count_y * count_z, kept_y * kept_z, 2).astype(jnp.bfloat16)


def line_table(full_length, kept_count):
    freq_x = frequencies(kept_count, full_length)
    turns = jnp.arange(full_length, dtype=jnp.int32)[:, None] * freq_x[None, :] % full_length
    angles = 2.0 * math.pi * turns.astype(jnp.float32) / full_length
    factor = 1.0 / math.sqrt(full_length)
    cos_part = factor * jnp.cos(angles)
    sine_part = factor * jnp.sin(angles)
    first_row = jnp.stack([cos_part, -sine_part], axis=1)
    second = jnp.stack([sine_part, cos_part], axis=1)
    return jnp.stack([first_row, second], axis=0).astype(jnp.bfloat16)


def mode_doubling(kept_y, kept_z):
    mode_index = jnp.arange(kept_y * kept_z, dtype=jnp.int32) % kept_z
    return jnp.where(mode_index == 0, 1.0, 2.0).astype(jnp.float32)


def gelu_slope(values):
    inner_arg = tanh_coef * (values + cubic_coef * values * values * values)
    tanh_part = jnp.tanh(inner_arg)
    return 0.5 * (1.0 + tanh_part) + 0.5 * values * (1.0 - tanh_part * tanh_part) * tanh_coef * (
        1.0 + 3.0 * cubic_coef * values * values
    )


def product(equation, left_op, right_op):
    return jnp.einsum(equation, left_op, right_op, preferred_element_type=jnp.float32)


def forward_lines(coarse, line_basis):
    return product("xpscm,pxqk->kqscm", coarse, line_basis).astype(jnp.bfloat16)


def inverse_lines(spectrum, line_basis):
    return product("kqscm,pxqk->xpscm", spectrum, line_basis).astype(jnp.bfloat16)


def spectral_mix(spectrum, weights):
    real_part = spectrum[:, 0]
    imag_part = spectrum[:, 1]
    w_real = weights[:, :, 0]
    w_imag = weights[:, :, 1]
    out_real = product("ksim,mkio->ksom", real_part, w_real) - product(
        "ksim,mkio->ksom", imag_part, w_imag
    )
    out_imag = product("ksim,mkio->ksom", real_part, w_imag) + product(
        "ksim,mkio->ksom", imag_part, w_real
    )
    return jnp.stack([out_real, out_imag], axis=1).astype(jnp.bfloat16)


def spectral_pull(adjoint, weights):
    real_part = adjoint[:, 0]
    imag_part = adjoint[:, 1]
    w_real = weights[:, :, 0]
    w_imag = weights[:, :, 1]
    out_real = product("ksom,mkio->ksim", real_part, w_real) + product(
        "ksom,mkio->ksim", imag_part, w_imag
    )
    out_imag = product("ksom,mkio->ksim", imag_part, w_real) - product(
        "ksom,mkio->ksim", real_part, w_imag
    )
    return jnp.stack([out_real, out_imag], axis=1).astype(jnp.bfloat16)


def weight_grad(spectrum, adjoint):
    spec_real = spectrum[:, 0]
    spec_imag = spectrum[:, 1]
    adj_real = adjoint[:, 0]
    adj_imag = adjoint[:, 1]
    grad_real = product("ksim,ksom->mkio", spec_real, adj_real) + product(
        "ksim,ksom->mkio", spec_imag, adj_imag
    )
    grad_imag = product("ksim,ksom->mkio", spec_real, adj_imag) - product(
        "ksim,ksom->mkio", spec_imag, adj_real
    )
    return jnp.stack([grad_real, grad_imag], axis=2)


def to_modes(coarse):
    return lax.all_to_all(coarse, "space", split_axis=4, concat_axis=0, tiled=True)


def to_cells(returned):
    return lax.all_to_all(returned, "space", split_axis=0, concat_axis=4, tiled=True)


def body(features, cotangent, spectral, pointwise, biases):
    samples, channels, slab_cells, span_y, span_z = features.shape
    full_length = slab_cells * lax.axis_size("space")
    plane_basis = plane_table(span_y, span_z, KY, KZ)
    line_basis = line_table(full_length, KX)
    doubling = mode_doubling(KY, KZ)
    doubling_cells = doubling.astype(jnp.bfloat16)[None, None, None, None, :]
    flat_cells = features.reshape(samples, channels, slab_cells, span_y * span_z)
    coarse = product("scxq,qmp->xpscm", flat_cells, plane_basis).astype(jnp.bfloat16)
    spectrum = forward_lines(to_modes(coarse), line_basis)
    local_modes = spectral.shape[0]
    blocks = lax.all_gather(spectral, "dp", axis=1, tiled=True)
    weights = blocks.reshape(local_modes, blocks.shape[1], 2, channels, channels)
    mixed_modes = spectral_mix(spectrum, weights)
    returned = to_cells(inverse_lines(mixed_modes, line_basis))
    spectral_part = product("xpscm,qmp->scxq", returned * doubling_cells, plane_basis)
    linear = product("sicq,io->socq", flat_cells, pointwise)
    pre_act = linear + biases.astype(jnp.float32)[None, :, None, None] + spectral_part
    upstream_grad = cotangent.reshape(flat_cells.shape).astype(jnp.float32)
    delta_cells = (upstream_grad * gelu_slope(pre_act)).astype(jnp.bfloat16)
    coarse_back = (
        product("scxq,qmp->xpscm", delta_cells, plane_basis) * doubling[None, None, None, None, :]
    ).astype(jnp.bfloat16)
    adjoint = forward_lines(to_modes(coarse_back), line_basis)
    pulled = spectral_pull(adjoint, weights)
    grad_terms = weight_grad(spectrum, adjoint)
    grad_spectral = lax.psum_scatter(
        grad_terms.reshape(local_modes, KX, 2 * channels * channels).astype(jnp.bfloat16),
        "dp",
        scatter_dimension=1,
        tiled=True,
    ).astype(jnp.float32)
    back_cells = to_cells(inverse_lines(pulled, line_basis))
    grad_cells = product("socq,io->sicq", delta_cells, pointwise) + product(
        "xpscm,qmp->scxq", back_cells, plane_basis
    )
    grad_input = grad_cells.astype(jnp.bfloat16).reshape(features.shape)
    return (grad_input, grad_spectral)


def solution(mesh):
    placed = (
        P("dp", None, "space", None, None),
        P("dp", None, "space", None, None),
        P("space", "dp", None),
        P(),
        P(),
    )
    return jax.shard_map(
        body,
        mesh=mesh,
        in_specs=placed,
        out_specs=(P("dp", None, "space", None, None), P("space", "dp", None)),
        check_vma=False,
    )
```

profile of v0, /device:TPU:1, one launch (start us, length us, event | category | flops | bytes accessed | tf_op | source)
XLA Modules:
  0.0 200.6 jit_solution(17120328328237646972)
XLA Ops:
  7.2 1.5 copy.54
  8.7 1.3 reshape.427
  10.1 17.5 %multiply_convert_fusion.1 = (bf16[32,128,32,8]{1,0,3,2:T(8,128)(2,1)S(1)}, bf16[32,128,32,8]{1,0,3,2:T(8,128)(2,1)}) fusion(f32[128,8]{0,1:T(8,128)S(1)} %fusion.108, f32[32,32]{0,1:T(8,128)S(1)} %fusion.92), kind=kLoop, calls=%fused_computation.19 | loop fusion | flops 6291456 | bytes 4202496 | tf_op jit(solution)/shard_map/convert.44
  27.6 4.2 %mul.256 = bf16[4096,256,1]{0,1,2:T(8,128)(2,1)} reshape(bf16[32,128,32,8]{1,0,3,2:T(8,128)(2,1)} %get-tuple-element.19) | data formatting | bytes 4194304 | tf_op jit(solution)/shard_map/mul | solution.py:36
  31.8 4.1 %copy.47 = bf16[4096,256,1]{1,0,2:T(8,128)(2,1)} copy(bf16[4096,256,1]{0,1,2:T(8,128)(2,1)} %mul.256) | data formatting | bytes 4194304 | tf_op jit(solution)/shard_map/mul | solution.py:36
  35.9 2.3 %mul.253 = bf16[4096,256,1]{0,1,2:T(8,128)(2,1)} reshape(bf16[32,128,32,8]{1,0,3,2:T(8,128)(2,1)S(1)} %get-tuple-element.18) | data formatting | bytes 4194304 | tf_op jit(solution)/shard_map/mul | solution.py:36
  38.3 4.3 %copy.46 = bf16[4096,256,1]{1,0,2:T(8,128)(2,1)} copy(bf16[4096,256,1]{0,1,2:T(8,128)(2,1)} %mul.253) | data formatting | bytes 4194304 | tf_op jit(solution)/shard_map/mul | solution.py:36
  42.5 2.7 %fusion.45 = bf16[4,2,1,32,256]{4,3,0,1,2:T(8,128)(2,1)S(1)} fusion(bf16[32,4,4096]{2,1,0:T(4,128)(2,1)S(1)} %reshape.427, bf16[4096,256,1]{1,0,2:T(8,128)(2,1)S(1)} %copy-done.3, bf16[4096,256,1]{1,0,2:T(8,128)(2,1)} %copy.46), kind=kOutput, calls=%fused_computation.54 | convolution fusion | flops 545325056 | bytes 5373952 | tf_op jit(solution)/shard_map/scxq,qmp->xpscm/dot_general | solution.py:66
  45.2 0.3 copy.50
  45.6 1.2 reshape.470
  46.8 10.5 %all-to-all-start = ((bf16[32,2,1024]{2,1,0:T(2,128)(2,1)}), bf16[32,2,1024]{2,1,0:T(2,128)(2,1)S(1)}, u32[]{:S(2)}, u32[]{:S(2)}) async-start(bf16[32,2,1024]{2,1,0:T(2,128)(2,1)} %reshape.470), calls=%async_computation | async-start | bytes 262144 | tf_op jit(solution)/shard_map/all_to_all | solution.py:120
  57.3 0.2 negate_convert_fusion
  57.4 1.7 reshape.469
  59.2 7.2 %all-to-all-done = bf16[32,2,1024]{2,1,0:T(2,128)(2,1)S(1)} async-done(((bf16[32,2,1024]{2,1,0:T(2,128)(2,1)}), bf16[32,2,1024]{2,1,0:T(2,128)(2,1)S(1)}, u32[]{:S(2)}, u32[]{:S(2)}) %all-to-all-start) | async-done | bytes 131104 | tf_op jit(solution)/shard_map/all_to_all | solution.py:120
  66.4 0.3 reshape.471
  66.8 0.1 copy.52
  66.9 0.5 copy.53
  67.3 0.2 fusion.51
  67.7 5.9 %reshape.430 = bf16[8,32,2,32,32]{4,3,2,0,1:T(8,128)(2,1)} reshape(bf16[8,32,2048]{2,0,1:T(8,128)(2,1)} %all-gather.2.cloned.1.call-done) | data formatting | bytes 2097152 | tf_op jit(solution)/shard_map/reshape | solution.py:139
  73.6 2.4 %fusion.28 = f32[32,8,1,32]{3,2,1,0:T(1,128)S(1)} fusion(bf16[8,32,2,32,32]{4,3,2,0,1:T(8,128)(2,1)} %reshape.430, bf16[32,32,8,1]{1,0,2,3:T(8,128)(2,1)S(1)} %get-tuple-element.12), kind=kOutput, calls=%fused_computation.41 | convolution fusion | flops 524288 | bytes 2146304 | tf_op jit(solution)/shard_map/ksim,mkio->ksom/dot_general | solution.py:66
  76.0 2.3 %fusion.23 = f32[32,8,1,32]{3,2,1,0:T(1,128)S(1)} fusion(bf16[8,32,2,32,32]{4,3,2,0,1:T(8,128)(2,1)} %reshape.430, bf16[32,32,8,1]{1,0,2,3:T(8,128)(2,1)S(1)} %get-tuple-element.12), kind=kOutput, calls=%fused_computation.36 | convolution fusion | flops 524288 | bytes 2146304 | tf_op jit(solution)/shard_map/ksim,mkio->ksom/dot_general | solution.py:66
  78.3 0.7 fusion.24
  79.0 0.7 fusion.27
  80.2 0.2 fusion.50
  80.4 0.4 copy.56
  80.9 1.2 reshape.472
  82.1 4.2 %all-to-all-start.1 = ((bf16[32,2,1024]{2,1,0:T(2,128)(2,1)}), bf16[32,2,1024]{2,1,0:T(2,128)(2,1)S(1)}, u32[]{:S(2)}, u32[]{:S(2)}) async-start(bf16[32,2,1024]{2,1,0:T(2,128)(2,1)} %reshape.472), calls=%async_computation.1 | async-start | bytes 262144 | tf_op jit(solution)/shard_map/all_to_all | solution.py:124
  86.2 0.5 fusion.112
  86.8 2.9 %fusion.2 = f32[1,32,4,4096]{3,1,2,0:T(8,128)} fusion(f32[32]{0:T(128)S(1)} %convert_element_type.144, bf16[32,4,4096]{2,1,0:T(4,128)(2,1)S(1)} %reshape.427, bf16[32,32]{1,0:T(8,128)(2,1)S(1)} %copy-done), kind=kOutput, calls=%fused_computation.6 | convolution fusion | flops 34078720 | bytes 3147904 | tf_op jit(solution)/shard_map/sicq,io->socq/dot_general | solution.py:66
  89.7 5.5 %all-to-all-done.1 = bf16[32,2,1024]{2,1,0:T(2,128)(2,1)S(1)} async-done(((bf16[32,2,1024]{2,1,0:T(2,128)(2,1)}), bf16[32,2,1024]{2,1,0:T(2,128)(2,1)S(1)}, u32[]{:S(2)}, u32[]{:S(2)}) %all-to-all-start.1) | async-done | bytes 131104 | tf_op jit(solution)/shard_map/all_to_all | solution.py:124
  95.2 1.0 reshape.473
  96.2 6.2 %fusion.16 = bf16[1,32,4,4096]{3,1,2,0:T(8,128)(2,1)S(1)} fusion(f32[1,32,4,4096]{3,2,1,0:T(4,128)S(1)} %copy-done.2, f32[1,32,4,4096]{3,1,2,0:T(8,128)} %fusion.2, bf16[4,2,1,32,32,8]{3,5,1,0,4,2:T(8,128)(2,1)} %bitcast.327, bf16[256]{0:T(256)(128)(2,1)} %fusion.112, bf16[4096,256,1]{1,0,2:T(8,128)(2,1)} %copy.47, bf16[4096,256,1]{1,0,2:T(8,128)(2,1)} %copy.46), kind=kOutput, calls=%fused_computation.29 | convolution fusion | flops 556007424 | bytes 9568768 | tf_op jit(solution)/shard_map/xpscm,qmp->scxq/dot_general | solution.py:66
  102.5 0.8 fusion.52
  103.3 0.3 copy.59
  103.6 1.2 reshape.474
  104.8 4.0 %all-to-all-start.2 = ((bf16[32,2,1024]{2,1,0:T(2,128)(2,1)}), bf16[32,2,1024]{2,1,0:T(2,128)(2,1)S(1)}, u32[]{:S(2)}, u32[]{:S(2)}) async-start(bf16[32,2,1024]{2,1,0:T(2,128)(2,1)} %reshape.474), calls=%async_computation.2 | async-start | bytes 262144 | tf_op jit(solution)/shard_map/all_to_all | solution.py:120
  109.0 8.9 %all-to-all-done.2 = bf16[32,2,1024]{2,1,0:T(2,128)(2,1)S(1)} async-done(((bf16[32,2,1024]{2,1,0:T(2,128)(2,1)}), bf16[32,2,1024]{2,1,0:T(2,128)(2,1)S(1)}, u32[]{:S(2)}, u32[]{:S(2)}) %all-to-all-start.2) | async-done | bytes 131104 | tf_op jit(solution)/shard_map/all_to_all | solution.py:120
  117.9 0.3 reshape.475
  118.3 0.1 copy.61
  118.4 0.5 copy.62
  118.9 0.2 fusion.49
  119.4 2.5 %fusion.17 = (bf16[8,32,1,32,32]{4,3,2,0,1:T(8,128)(2,1)S(1)}, bf16[8,32,1,32,32]{4,3,2,0,1:T(8,128)(2,1)S(1)}) fusion(f32[8,32,32]{2,0,1:T(8,128)S(1)} %copy.70, f32[8,32,32]{2,0,1:T(8,128)S(1)} %copy.69, f32[8,32,32]{2,0,1:T(8,128)S(1)} %copy.68, f32[8,32,32]{2,0,1:T(8,128)S(1)} %copy.67), kind=kLoop, calls=%fused_computation.30 | loop fusion | flops 2097152 | bytes 1179648 | tf_op jit(solution)/shard_map/stack | solution.py:116
  121.8 2.8 %pad_maximum_fusion.1 = bf16[8,32,2,32,32]{4,3,2,0,1:T(8,128)(2,1)} fusion(bf16[8,32,1,32,32]{4,3,2,0,1:T(8,128)(2,1)S(1)} %get-tuple-element.9, bf16[8,32,1,32,32]{4,3,2,0,1:T(8,128)(2,1)S(1)} %get-tuple-element.8), kind=kLoop, calls=%fused_computation.9 | loop fusion | flops 524288 | bytes 2097152 | tf_op jit(solution)/shard_map/stack | solution.py:116
  124.7 6.8 %convert_element_type.168 = bf16[8,32,2048]{2,0,1:T(8,128)(2,1)} reshape(bf16[8,32,2,32,32]{4,3,2,0,1:T(8,128)(2,1)} %pad_maximum_fusion.1) | data formatting | bytes 2097152 | tf_op jit(solution)/shard_map/convert_element_type | solution.py:154
  131.5 2.8 %fusion.25 = f32[32,8,1,32]{3,2,1,0:T(1,128)S(1)} fusion(bf16[8,32,2,32,32]{4,3,2,0,1:T(8,128)(2,1)} %reshape.430, bf16[32,32,8,1]{1,0,2,3:T(8,128)(2,1)S(1)} %get-tuple-element.15), kind=kOutput, calls=%fused_computation.38 | convolution fusion | flops 524288 | bytes 2146304 | tf_op jit(solution)/shard_map/ksom,mkio->ksim/dot_general | solution.py:66
  134.3 0.1 copy.94
  134.4 2.8 %fusion.21 = f32[32,8,1,32]{3,2,1,0:T(1,128)S(1)} fusion(bf16[8,32,2,32,32]{4,3,2,0,1:T(8,128)(2,1)} %reshape.430, bf16[32,32,8,1]{1,0,2,3:T(8,128)(2,1)S(1)} %get-tuple-element.16), kind=kOutput, calls=%fused_computation.34 | convolution fusion | flops 524288 | bytes 2146304 | tf_op jit(solution)/shard_map/ksom,mkio->ksim/dot_general | solution.py:66
  137.2 0.1 copy.93
  137.4 2.8 %fusion.26 = f32[32,8,1,32]{3,2,1,0:T(1,128)S(1)} fusion(bf16[8,32,2,32,32]{4,3,2,0,1:T(8,128)(2,1)} %reshape.430, bf16[32,32,8,1]{1,0,2,3:T(8,128)(2,1)S(1)} %get-tuple-element.16), kind=kOutput, calls=%fused_computation.39 | convolution fusion | flops 524288 | bytes 2146304 | tf_op jit(solution)/shard_map/ksom,mkio->ksim/dot_general | solution.py:66
  140.2 0.1 copy.92
  140.3 2.8 %fusion.22 = f32[32,8,1,32]{3,2,1,0:T(1,128)S(1)} fusion(bf16[8,32,2,32,32]{4,3,2,0,1:T(8,128)(2,1)} %reshape.430, bf16[32,32,8,1]{1,0,2,3:T(8,128)(2,1)S(1)} %get-tuple-element.15), kind=kOutput, calls=%fused_computation.35 | convolution fusion | flops 524288 | bytes 2146304 | tf_op jit(solution)/shard_map/ksom,mkio->ksim/dot_general | solution.py:66
  143.1 0.1 copy.90
  143.3 0.2 fusion.48
  143.6 0.4 copy.64
  144.0 1.2 reshape.476
  145.2 3.9 %all-to-all-start.3 = ((bf16[32,2,1024]{2,1,0:T(2,128)(2,1)}), bf16[32,2,1024]{2,1,0:T(2,128)(2,1)S(1)}, u32[]{:S(2)}, u32[]{:S(2)}) async-start(bf16[32,2,1024]{2,1,0:T(2,128)(2,1)} %reshape.476), calls=%async_computation.3 | async-start | bytes 262144 | tf_op jit(solution)/shard_map/all_to_all | solution.py:124
  149.0 0.4 convolution_bitcast_fusion
  149.5 8.7 %all-to-all-done.3 = bf16[32,2,1024]{2,1,0:T(2,128)(2,1)S(1)} async-done(((bf16[32,2,1024]{2,1,0:T(2,128)(2,1)}), bf16[32,2,1024]{2,1,0:T(2,128)(2,1)S(1)}, u32[]{:S(2)}, u32[]{:S(2)}) %all-to-all-start.3) | async-done | bytes 131104 | tf_op jit(solution)/shard_map/all_to_all | solution.py:124
  158.2 0.3 reshape.477
  158.4 3.8 %fusion.3 = bf16[1,32,4,4096]{3,1,2,0:T(8,128)(2,1)S(1)} fusion(f32[1,32,4,4096]{3,1,2,0:T(8,128)S(1)} %convolution_bitcast_fusion, bf16[4,2,1,32,32,8]{3,5,1,0,4,2:T(8,128)(2,1)S(1)} %bitcast.328, bf16[4096,256,1]{1,0,2:T(8,128)(2,1)} %copy.47, bf16[4096,256,1]{1,0,2:T(8,128)(2,1)} %copy.46), kind=kOutput, calls=%fused_computation.7 | convolution fusion | flops 546308096 | bytes 7471104 | tf_op jit(solution)/shard_map/xpscm,qmp->scxq/dot_general | solution.py:66
  162.2 0.2 copy.105
  162.5 1.1 copy.72
  163.6 28.6 %reduce-scatter.2.cloned.1.call-done = bf16[8,2,2048]{2,0,1:T(8,128)(2,1)} async-done(((bf16[8,32,2048]{2,0,1:T(8,128)(2,1)}), bf16[8,2,2048]{2,0,1:T(8,128)(2,1)}) %reduce-scatter.2.cloned.1.call-update) | async-done | bytes 65552 | tf_op jit(solution)/shard_map/reduce_scatter | solution.py:153
  192.2 1.6 copy.73
  (50 shorter events, 1.3 us)
Async XLA Ops:
  7.2 79.6 %copy-start = (bf16[32,32]{1,0:T(8,128)(2,1)S(1)}, bf16[32,32]{1,0:T(8,128)(2,1)}, u32[]{:S(2)}) copy-start(bf16[32,32]{1,0:T(8,128)(2,1)} %param.8) | copy-start | bytes 6148
  7.2 60.5 %all-gather.2.cloned.1.call-start = ((), (), s32[]{:S(2)}) async-start(), calls=%async_computation.5 | async-start | bytes 1114112 | tf_op jit(solution)/shard_map/all_gather | solution.py:138
  38.2 4.3 %copy-start.3 = (bf16[4096,256,1]{1,0,2:T(8,128)(2,1)S(1)}, bf16[4096,256,1]{1,0,2:T(8,128)(2,1)}, u32[]{:S(2)}) copy-start(bf16[4096,256,1]{1,0,2:T(8,128)(2,1)} %copy.47) | copy-start | bytes 6291460
  45.2 12.2 %copy-start.6 = (bf16[1,32,4,32,128]{4,3,2,1,0:T(8,128)(2,1)S(1)}, bf16[1,32,4,32,128]{4,3,2,1,0:T(8,128)(2,1)}, u32[]{:S(2)}) copy-start(bf16[1,32,4,32,128]{4,3,2,1,0:T(8,128)(2,1)} %param.6) | copy-start | bytes 3145732
  45.6 13.6 %copy-start.11 = (bf16[32]{0:T(256)(128)(2,1)S(1)}, bf16[32]{0:T(256)(128)(2,1)}, u32[]{:S(2)}) copy-start(bf16[32]{0:T(256)(128)(2,1)} %param.9) | copy-start | bytes 196
  46.8 19.6 %all-to-all-start = ((bf16[32,2,1024]{2,1,0:T(2,128)(2,1)}), bf16[32,2,1024]{2,1,0:T(2,128)(2,1)S(1)}, u32[]{:S(2)}, u32[]{:S(2)}) async-start(bf16[32,2,1024]{2,1,0:T(2,128)(2,1)} %reshape.470), calls=%async_computation | async-start | bytes 262144 | tf_op jit(solution)/shard_map/all_to_all | solution.py:120
  59.2 21.0 %copy-start.7 = (bf16[1,128,2,32]{1,3,0,2:T(8,128)(2,1)}, bf16[1,128,2,32]{1,3,0,2:T(8,128)(2,1)S(1)}, u32[]{:S(2)}) copy-start(bf16[1,128,2,32]{1,3,0,2:T(8,128)(2,1)S(1)} %get-tuple-element.20) | copy-start | bytes 49156
  59.2 21.0 %copy-start.9 = (bf16[1,128,2,32]{1,3,0,2:T(8,128)(2,1)}, bf16[1,128,2,32]{1,3,0,2:T(8,128)(2,1)S(1)}, u32[]{:S(2)}) copy-start(bf16[1,128,2,32]{1,3,0,2:T(8,128)(2,1)S(1)} %get-tuple-element.21) | copy-start | bytes 49156
  73.6 4.7 %copy-start.1 = (bf16[8,32,2,32,32]{4,3,2,0,1:T(8,128)(2,1)S(1)}, bf16[8,32,2,32,32]{4,3,2,0,1:T(8,128)(2,1)}, u32[]{:S(2)}) copy-start(bf16[8,32,2,32,32]{4,3,2,0,1:T(8,128)(2,1)} %reshape.430) | copy-start | bytes 3145732
  82.0 14.2 %copy-start.2 = (f32[1,32,4,4096]{3,2,1,0:T(4,128)S(1)}, f32[1,32,4,4096]{3,2,1,0:T(4,128)}, u32[]{:S(2)}) copy-start(f32[1,32,4,4096]{3,2,1,0:T(4,128)} %reshape.469) | copy-start | bytes 6291460
  82.1 13.1 %all-to-all-start.1 = ((bf16[32,2,1024]{2,1,0:T(2,128)(2,1)}), bf16[32,2,1024]{2,1,0:T(2,128)(2,1)S(1)}, u32[]{:S(2)}, u32[]{:S(2)}) async-start(bf16[32,2,1024]{2,1,0:T(2,128)(2,1)} %reshape.472), calls=%async_computation.1 | async-start | bytes 262144 | tf_op jit(solution)/shard_map/all_to_all | solution.py:124
  96.2 6.3 %copy-start.4 = (bf16[4096,256,1]{1,0,2:T(8,128)(2,1)S(1)}, bf16[4096,256,1]{1,0,2:T(8,128)(2,1)}, u32[]{:S(2)}) copy-start(bf16[4096,256,1]{1,0,2:T(8,128)(2,1)} %copy.47) | copy-start | bytes 6291460
  96.2 6.3 %copy-start.5 = (bf16[4096,256,1]{1,0,2:T(8,128)(2,1)S(1)}, bf16[4096,256,1]{1,0,2:T(8,128)(2,1)}, u32[]{:S(2)}) copy-start(bf16[4096,256,1]{1,0,2:T(8,128)(2,1)} %copy.46) | copy-start | bytes 6291460
  104.8 14.1 %copy-start.8 = (bf16[1,128,2,32]{1,3,0,2:T(8,128)(2,1)S(1)}, bf16[1,128,2,32]{1,3,0,2:T(8,128)(2,1)}, u32[]{:S(2)}) copy-start(bf16[1,128,2,32]{1,3,0,2:T(8,128)(2,1)} %copy-done.7) | copy-start | bytes 49156
  104.8 14.1 %copy-start.10 = (bf16[1,128,2,32]{1,3,0,2:T(8,128)(2,1)S(1)}, bf16[1,128,2,32]{1,3,0,2:T(8,128)(2,1)}, u32[]{:S(2)}) copy-start(bf16[1,128,2,32]{1,3,0,2:T(8,128)(2,1)} %copy-done.9) | copy-start | bytes 49156
  104.8 13.1 %all-to-all-start.2 = ((bf16[32,2,1024]{2,1,0:T(2,128)(2,1)}), bf16[32,2,1024]{2,1,0:T(2,128)(2,1)S(1)}, u32[]{:S(2)}, u32[]{:S(2)}) async-start(bf16[32,2,1024]{2,1,0:T(2,128)(2,1)} %reshape.474), calls=%async_computation.2 | async-start | bytes 262144 | tf_op jit(solution)/shard_map/all_to_all | solution.py:120
  108.8 83.4 %reduce-scatter.2.cloned.1.call-start = ((), (), s32[]{:S(2)}) async-start(), calls=%async_computation.6 | async-start | bytes 1114112 | tf_op jit(solution)/shard_map/reduce_scatter | solution.py:153
  145.2 13.0 %all-to-all-start.3 = ((bf16[32,2,1024]{2,1,0:T(2,128)(2,1)}), bf16[32,2,1024]{2,1,0:T(2,128)(2,1)S(1)}, u32[]{:S(2)}, u32[]{:S(2)}) async-start(bf16[32,2,1024]{2,1,0:T(2,128)(2,1)} %reshape.476), calls=%async_computation.3 | async-start | bytes 262144 | tf_op jit(solution)/shard_map/all_to_all | solution.py:124
Sparse Core Ops, SparseCore 0:
  10.7 47.8 all-gather.1
  131.6 60.4 reduce-scatter.1
where the time goes:
time: 204 us; the launch traced here: 201 us
  waiting for transfers between devices  59 us (29%)
  local copies, waits for them, and re-layouts  45.8 us (22%)
  matrix products  35 us (17%)
  other arithmetic  23.7 us (12%)
  starting transfers between devices  22.6 us (11%)
  between operations  14.5 us (7%)
    dot_general x18, matrix products, product(): jnp.einsum(equation, left_op, right_op, preferred_element_type=jnp.float32)  35 us
    reduce_scatter x1, waiting for transfers between devices, body(): lax.psum_scatter(grad_terms.reshape(local_modes, KX, 2 * channels * chann...  28.6 us
    another operation x4, other arithmetic  17.8 us
    all_to_all x2, waiting for transfers between devices, to_modes(): lax.all_to_all(coarse, 'space', split_axis=4, concat_axis=0, tiled=True)  16.1 us
    all_to_all x2, starting transfers between devices, to_modes(): lax.all_to_all(coarse, 'space', split_axis=4, concat_axis=0, tiled=True)  14.5 us
    all_to_all x2, waiting for transfers between devices, to_cells(): lax.all_to_all(returned, 'space', split_axis=0, concat_axis=4, tiled=True)  14.2 us
    unnamed x36, local copies, waits for them, and re-layouts  11 us
    mul x2, local copies, waits for them, and re-layouts, plane_table(): -factor * jnp.sin(angles)  8.29 us
  transfers between devices with their start and end apart: 6, of which 5 were waited for; matrix products, arithmetic and copies ran while one was open for 32% of the time, Pallas kernels for 0%

commit v1 on v0

v1 whole, which is shorter than its diff:
```python
import math

import numpy as np
import jax
import jax.numpy as jnp
from jax import lax
from jax.experimental import pallas as pl
from jax.experimental.pallas import tpu as pltpu
from jax.sharding import PartitionSpec as P

KX = 32
KY = 32
KZ = 8
NY = 32
NZ = 128
NX = 128
C = 32
SLAB = 4
STEPS = 15

tanh_coef = 0.7978845608028654
cubic_coef = 0.044715

F32 = jnp.float32
BF16 = jnp.bfloat16


def frequencies(kept_count, length):
    indices = np.arange(kept_count, dtype=np.int32)
    return np.where(indices < kept_count // 2, indices, indices + (length - kept_count)).astype(np.int32)


def plane_table():
    freq_y = frequencies(KY, NY)
    freq_z = np.arange(KZ, dtype=np.int32)
    ys = np.array(list(range(1, 16)) + [0, 16], dtype=np.int32)
    turn_y = ys[:, None] * freq_y[None, :] % NY
    turn_z = np.arange(NZ, dtype=np.int32)[:, None] * freq_z[None, :] % NZ
    angles = np.float32(2.0 * math.pi) * (
        turn_y[:, None, :, None].astype(np.float32) / np.float32(NY)
        + turn_z[None, :, None, :].astype(np.float32) / np.float32(NZ)
    )
    factor = np.float32(1.0 / math.sqrt(NY * NZ))
    table = np.stack([factor * np.cos(angles), -factor * np.sin(angles)], axis=-1)
    table = table.reshape(17, NZ, KY, 2, 4, 2).transpose(2, 4, 3, 5, 0, 1)
    return table.reshape(KY * KZ * 2, 17 * NZ).astype(BF16)


def line_table():
    freq_x = frequencies(KX, NX)
    turns = np.arange(NX, dtype=np.int32)[:, None] * freq_x[None, :] % NX
    angles = np.float32(2.0 * math.pi) * turns.astype(np.float32) / np.float32(NX)
    factor = np.float32(1.0 / math.sqrt(NX))
    cos_part = factor * np.cos(angles)
    sine_part = factor * np.sin(angles)
    first_row = np.stack([cos_part, -sine_part], axis=1)
    second = np.stack([sine_part, cos_part], axis=1)
    line = np.stack([first_row, second], axis=0)
    line = line.reshape(2, 32, 4, 2, 16, 2).transpose(4, 3, 5, 1, 2, 0)
    full = np.zeros((16, 2, 2, 2, 32, 4, 2, 2), np.float32)
    for hi in range(2):
        full[:, :, hi, :, :, :, hi, :] = line
    return full.reshape(128, 512).astype(BF16)


def gelu_slope(values):
    inner_arg = tanh_coef * (values + cubic_coef * values * values * values)
    tanh_part = jnp.tanh(inner_arg)
    return 0.5 * (1.0 + tanh_part) + 0.5 * values * (1.0 - tanh_part * tanh_part) * tanh_coef * (
        1.0 + 3.0 * cubic_coef * values * values
    )


def dot(left, right, dims=((1,), (0,))):
    return lax.dot_general(left, right, (dims, ((), ())), preferred_element_type=F32)


def iota(shape, axis):
    return lax.broadcasted_iota(jnp.int32, shape, axis)


def as_bf16(condition):
    return jnp.where(condition, 1.0, 0.0).astype(BF16)


def swap_blocks(value):
    v = value.reshape(64, 8, 128)
    row_low = iota((1, 8, 128), 1) >> 2
    lane = iota((1, 8, 128), 2) >> 5
    lane_low = lane & 1
    lane_high = lane >> 1
    turned = pltpu.roll(v, 4, 1)
    up = pltpu.roll(turned, 32, 2)
    down = pltpu.roll(turned, 96, 2)
    v = jnp.where(row_low == lane_low, v, jnp.where(lane_low == 1, up, down))
    v = v.reshape(32, 2, 8, 128)
    first, second = v[:, 0], v[:, 1]
    new_first = jnp.where(lane_high == 0, first, pltpu.roll(second, 64, 2))
    new_second = jnp.where(lane_high == 1, second, pltpu.roll(first, 64, 2))
    return jnp.stack([new_first, new_second], axis=1).reshape(512, 128)


def negate_jy(value):
    return jnp.concatenate([value[16 * ((32 - j) % 32) : 16 * ((32 - j) % 32) + 16] for j in range(32)], axis=0)


def doubled(value):
    jz = iota(value.shape, 0) & 14
    return value * jnp.where(jz == 0, 1.0, 2.0)


def gather_rows(wide, y):
    return jnp.concatenate(
        [wide[pl.ds(x * NY + y, C, stride=SLAB * NY), :] for x in range(SLAB)], axis=0
    )


def regroup(source_ref, wide, pairs_ref):
    wide[...] = source_ref[...].astype(F32)
    for s in range(1, 17):
        lanes = pl.ds((s - 1) * NZ, NZ)
        above, below = (0, 16) if s == 16 else (s, NY - s)
        pairs_ref[0:128, lanes] = gather_rows(wide, above).astype(BF16)
        pairs_ref[128:256, lanes] = gather_rows(wide, below).astype(BF16)


def to_coarse(table_ref, pairs_ref):
    last = slice(STEPS * NZ, 16 * NZ)
    both = dot(table_ref[:, 0 : STEPS * NZ], pairs_ref[:, 0 : STEPS * NZ], ((1,), (1,)))
    alone = dot(table_ref[:, last], pairs_ref[0:128, last], ((1,), (1,)))
    alone = alone + dot(table_ref[:, 16 * NZ : 17 * NZ], pairs_ref[128:256, last], ((1,), (1,)))
    return alone + both[:, 0:128] + negate_jy(both[:, 128:256])


def analyse_kernel(features_ref, table_ref, send_ref, pairs_out, wide, pairs_ref, sem):
    regroup(features_ref, wide, pairs_ref)
    copy = pltpu.make_async_copy(pairs_ref, pairs_out, sem)
    copy.start()
    coarse = to_coarse(table_ref, pairs_ref)
    send_ref[...] = swap_blocks(coarse).astype(BF16).reshape(32, 16, 128)
    copy.wait()


def regroup_kernel(source_ref, pairs_out, wide, pairs_ref, sem):
    regroup(source_ref, wide, pairs_ref)
    copy = pltpu.make_async_copy(pairs_ref, pairs_out, sem)
    copy.start()
    copy.wait()


def block_of(row):
    return ((row >> 7) & 1) * 8 + ((row >> 4) & 3) * 2 + ((row >> 6) & 1)


def repeat_kernel(spectral_ref, out_ref):
    rows = jnp.concatenate([spectral_ref[m].astype(F32) for m in range(8)], axis=0).astype(BF16)
    for z in range(8):
        out_ref[z] = rows


def weight_columns(low_ref, high_ref, start):
    lanes = slice(start, start + 128)
    return jnp.concatenate([low_ref[:, lanes], high_ref[:, lanes]], axis=0).astype(F32)


def spread_rows(compact):
    row = iota((512, 128), 0)
    wanted = block_of(row) * 8 + (row >> 8) * 4 + ((row >> 3) & 1) * 2 + (row & 1)
    select = as_bf16(wanted == iota((512, 128), 1))
    rows = dot(select, compact)
    return jnp.where((iota((512, 128), 1) >> 5) == ((row >> 1) & 3), rows, 0.0).astype(BF16)


def close_rows(rows):
    row = iota((512, 128), 0)
    kept = jnp.where((iota((512, 128), 1) >> 5) == ((row >> 1) & 3), rows, 0.0).astype(BF16)
    col = iota((128, 512), 1)
    wanted = block_of(col) * 8 + (col >> 8) * 4 + ((col >> 3) & 1) * 2 + (col & 1)
    select = as_bf16(wanted == iota((128, 512), 0))
    return dot(select, kept).astype(BF16)


def mix_kernel(recv_ref, low_ref, high_ref, line_ref, send_out, spec_out, send_ref, spec_ref, sems):
    compact = dot(line_ref[...], recv_ref[...].reshape(512, 128)).astype(BF16)
    spec_ref[...] = compact.astype(F32)
    spec_copy = pltpu.make_async_copy(spec_ref, spec_out, sems.at[0])
    spec_copy.start()
    rows = spread_rows(compact)
    out_real = jnp.zeros((256, 128), F32)
    out_imag = jnp.zeros((256, 128), F32)
    for t in range(8):
        spread = as_bf16((iota((128, 128), 0) & 31) == t * 4 + (iota((128, 128), 1) >> 5))
        wide = dot(rows, spread)
        s_real, s_imag = wide[0:256], wide[256:512]
        w_real = weight_columns(low_ref, high_ref, t * 128)
        w_imag = weight_columns(low_ref, high_ref, 1024 + t * 128)
        out_real = out_real + (s_real * w_real - s_imag * w_imag)
        out_imag = out_imag + (s_real * w_imag + s_imag * w_real)
    mixed = jnp.concatenate([out_real, out_imag], axis=0)
    mixed = mixed + pltpu.roll(mixed, 32, 1)
    mixed = mixed + pltpu.roll(mixed, 64, 1)
    compact = close_rows(mixed)
    send_ref[...] = dot(line_ref[...], compact, ((0,), (0,))).astype(BF16).reshape(32, 16, 128)
    send_copy = pltpu.make_async_copy(send_ref, send_out, sems.at[1])
    send_copy.start()
    spec_copy.wait()
    send_copy.wait()


def pull_kernel(recv_ref, low_ref, high_ref, line_ref, spec_ref, send_ref, pair_ref):
    compact = dot(line_ref[...], recv_ref[...].reshape(512, 128)).astype(BF16)
    pair_ref[...] = jnp.concatenate(
        [spec_ref[...].reshape(16, 8, 128), compact.astype(F32).reshape(16, 8, 128)], axis=1
    ).astype(BF16)
    rows = spread_rows(compact)
    repeat = as_bf16((iota((128, 128), 0) & 31) == (iota((128, 128), 1) & 31))
    wide = dot(rows, repeat)
    a_real, a_imag = wide[0:256], wide[256:512]
    pulled = jnp.zeros((512, 128), F32)
    for t in range(4):
        parts = []
        for u in range(2):
            w_real = weight_columns(low_ref, high_ref, (2 * t + u) * 128)
            w_imag = weight_columns(low_ref, high_ref, 1024 + (2 * t + u) * 128)
            parts.append(
                jnp.concatenate(
                    [a_real * w_real + a_imag * w_imag, a_imag * w_real - a_real * w_imag], axis=0
                ).astype(BF16)
            )
        collect = as_bf16((iota((256, 128), 0) >> 5) + t * 8 == (iota((256, 128), 1) & 31))
        pulled = pulled + dot(jnp.concatenate(parts, axis=1), collect)
    compact = close_rows(pulled)
    send_ref[...] = dot(line_ref[...], compact, ((0,), (0,))).astype(BF16).reshape(32, 16, 128)


def block_weights(weights_ref, transposed):
    spread = as_bf16((iota((256, 32), 0) & 31) == iota((256, 32), 1))
    dims = ((1,), (1,)) if transposed else ((1,), (0,))
    tall = dot(spread, weights_ref[...], dims).astype(BF16)
    full = dot(tall, spread, ((1,), (1,)))
    same = (iota((256, 256), 0) >> 5) == (iota((256, 256), 1) >> 5)
    return jnp.where(same, full, 0.0).astype(BF16), spread


def profiles(recv_ref, scale):
    value = swap_blocks(recv_ref[...].astype(F32).reshape(512, 128))
    if scale:
        value = doubled(value)
    both = jnp.concatenate([value, negate_jy(value)], axis=1)
    return both.T.astype(BF16)


def step_lanes():
    return [(2 * t * NZ, 2 * NZ) for t in range(7)] + [(14 * NZ, NZ)]


def nonlinear_kernel(
    recv_ref, table_ref, x_hbm, c_hbm, weights_ref, bias_ref, send_ref, delta_out, x_ref, c_ref, delta_ref, sems
):
    x_copy = pltpu.make_async_copy(x_hbm, x_ref, sems.at[0])
    x_copy.start()
    c_copy = pltpu.make_async_copy(c_hbm, c_ref, sems.at[1])
    c_copy.start()
    basis = profiles(recv_ref, True)
    mixing, spread = block_weights(weights_ref, True)
    bias = dot(spread, bias_ref[...])
    x_copy.wait()
    c_copy.wait()
    for start, width in step_lanes():
        lanes = slice(start, start + width)
        pre = dot(basis, table_ref[:, lanes]) + dot(mixing, x_ref[:, lanes]) + bias[:, 0:width]
        delta_ref[:, lanes] = (c_ref[:, lanes].astype(F32) * gelu_slope(pre)).astype(BF16)
    last = slice(STEPS * NZ, 16 * NZ)
    alone = jnp.concatenate(
        [dot(basis[0:128], table_ref[:, last]), dot(basis[0:128], table_ref[:, 16 * NZ : 17 * NZ])], axis=0
    )
    pre = alone + dot(mixing, x_ref[:, last]) + bias[:, 0:NZ]
    delta_ref[:, last] = (c_ref[:, last].astype(F32) * gelu_slope(pre)).astype(BF16)
    copy = pltpu.make_async_copy(delta_ref, delta_out, sems.at[2])
    copy.start()
    coarse = doubled(to_coarse(table_ref, delta_ref))
    send_ref[...] = swap_blocks(coarse).astype(BF16).reshape(32, 16, 128)
    copy.wait()


def input_grad_kernel(recv_ref, table_ref, delta_hbm, weights_ref, out_ref, wide, delta_ref, sem):
    copy = pltpu.make_async_copy(delta_hbm, delta_ref, sem)
    copy.start()
    basis = profiles(recv_ref, False)
    mixing, _ = block_weights(weights_ref, False)
    copy.wait()

    def put(value, y):
        for x in range(SLAB):
            wide[pl.ds(x * NY + y, C, stride=SLAB * NY), :] = value[x * C : x * C + C]

    for start, width in step_lanes():
        lanes = slice(start, start + width)
        grad = dot(basis, table_ref[:, lanes]) + dot(mixing, delta_ref[:, lanes])
        for u in range(width // NZ):
            s = start // NZ + u + 1
            put(grad[0:128, u * NZ : u * NZ + NZ], s)
            put(grad[128:256, u * NZ : u * NZ + NZ], NY - s)
    last = slice(STEPS * NZ, 16 * NZ)
    linear = dot(mixing, delta_ref[:, last])
    put(dot(basis[0:128], table_ref[:, last]) + linear[0:128], 0)
    put(dot(basis[0:128], table_ref[:, 16 * NZ : 17 * NZ]) + linear[128:256], 16)
    out_ref[...] = wide[...].astype(BF16)


def weight_grad_kernel(pair_ref, out_ref):
    row = iota((1024, 256), 0)
    wanted = ((row >> 4) & 15) * 16 + (row >> 9) * 8 + ((row >> 8) & 1) * 4 + ((row >> 3) & 1) * 2 + (row & 1)
    select = as_bf16(wanted == iota((1024, 256), 1))
    rows = dot(select, pair_ref[...].reshape(256, 128))
    row = iota((1024, 128), 0)
    rows = jnp.where((iota((1024, 128), 1) >> 5) == ((row >> 1) & 3), rows, 0.0).astype(BF16)
    repeat = as_bf16((iota((128, 128), 0) & 31) == (iota((128, 128), 1) & 31))
    wide = dot(rows[512:1024], repeat)
    a_real, a_imag = wide[0:256], wide[256:512]
    for t in range(8):
        spread = as_bf16((iota((128, 128), 0) & 31) == t * 4 + (iota((128, 128), 1) >> 5))
        wide = dot(rows[0:512], spread)
        s_real, s_imag = wide[0:256], wide[256:512]
        grad_real = jnp.sum((s_real * a_real + s_imag * a_imag).reshape(16, 16, 128), axis=0)
        grad_imag = jnp.sum((s_real * a_imag - s_imag * a_real).reshape(16, 16, 128), axis=0)
        for m in range(8):
            out_ref[m, :, t * 128 : t * 128 + 128] = grad_real[2 * m : 2 * m + 2]
            out_ref[m, :, 1024 + t * 128 : 1024 + t * 128 + 128] = grad_imag[2 * m : 2 * m + 2]


def run(kernel, name, outs, args, flops, scratch=(), out_hbm=(), in_hbm=()):
    args = [pltpu.with_memory_space_constraint(a, pltpu.HBM) if k in in_hbm else a for k, a in enumerate(args)]
    shapes = [(pltpu.HBM if k in out_hbm else jax.ShapeDtypeStruct)(*out) for k, out in enumerate(outs)]
    return pl.pallas_call(
        kernel,
        out_shape=shapes,
        in_specs=[
            pl.BlockSpec(memory_space=pltpu.HBM if k in in_hbm else pltpu.VMEM) for k in range(len(args))
        ],
        out_specs=[
            pl.BlockSpec(memory_space=pltpu.HBM if k in out_hbm else pltpu.VMEM) for k in range(len(outs))
        ],
        scratch_shapes=list(scratch),
        compiler_params=pltpu.CompilerParams(vmem_limit_bytes=32 * 2**20),
        cost_estimate=pl.CostEstimate(flops=flops, bytes_accessed=2 * 2**20, transcendentals=0),
        name=name,
    )(*args)


def exchange(value, axis):
    return lax.all_to_all(value, axis, split_axis=0, concat_axis=0, tiled=True)


def body(features, cotangent, spectral, pointwise, biases):
    table = jnp.asarray(plane_table())
    line = jnp.asarray(line_table())
    piece = ((32, 16, 128), BF16)
    pairs = ((256, 16 * NZ), BF16)
    wide = pltpu.VMEM((C * SLAB * NY, NZ), F32)
    held = pltpu.VMEM(*pairs)
    sem = pltpu.SemaphoreType.DMA(())

    same_core = [[2 * z + core for z in range(8)] for core in range(2)]
    same_chip = [[2 * z, 2 * z + 1] for z in range(8)]
    (copies,) = run(repeat_kernel, "repeat", [((8, 16, 2048), BF16)], [spectral], 10**6)
    blocks = lax.all_to_all(copies, "dp", 0, 0, tiled=True, axis_index_groups=same_core)
    send, x_pairs = run(
        analyse_kernel, "analyse", [piece, pairs], [features.reshape(C * SLAB * NY, NZ), table], 10**9,
        [wide, held, sem], (1,),
    )
    send, blocks = lax.optimization_barrier((send, blocks))
    w_low, w_high = (
        lax.all_gather(blocks[4 * h : 4 * h + 4], "dp", axis=0, tiled=True, axis_index_groups=same_chip).reshape(128, 2048)
        for h in range(2)
    )
    (c_pairs,) = run(
        regroup_kernel, "regroup", [pairs], [cotangent.reshape(C * SLAB * NY, NZ)], 10**6, [wide, held, sem], (0,)
    )
    send, spec = run(
        mix_kernel, "mix", [piece, ((128, 128), F32)], [exchange(send, "space"), w_low, w_high, line], 10**8,
        [pltpu.VMEM(*piece), pltpu.VMEM((128, 128), F32), pltpu.SemaphoreType.DMA((2,))], (0, 1),
    )
    bias = jnp.broadcast_to(biases[:, None], (C, 2 * NZ))
    send, delta = run(
        nonlinear_kernel, "nonlinear", [piece, pairs],
        [exchange(send, "space"), table, x_pairs, c_pairs, pointwise, bias], 2 * 10**9,
        [held, held, held, pltpu.SemaphoreType.DMA((3,))], (1,), (2, 3),
    )
    send, pair = run(
        pull_kernel, "pull", [piece, ((16, 16, 128), BF16)],
        [exchange(send, "space"), w_low, w_high, line, spec], 10**8,
    )
    recv = exchange(send, "space")
    pair, recv = lax.optimization_barrier((pair, recv))
    pair = exchange(pair, "dp")
    (grad_input,) = run(
        input_grad_kernel, "input_grad", [((C * SLAB * NY, NZ), BF16)],
        [recv, table, delta, pointwise], 10**9, [wide, held, sem], (), (2,),
    )
    (grad_spectral,) = run(weight_grad_kernel, "weight_grad", [((8, 2, 2048), F32)], [pair], 10**8)
    return grad_input.reshape(features.shape), grad_spectral


def solution(mesh):
    placed = (
        P("dp", None, "space", None, None),
        P("dp", None, "space", None, None),
        P("space", "dp", None),
        P(),
        P(),
    )
    return jax.shard_map(
        body,
        mesh=mesh,
        in_specs=placed,
        out_specs=(P("dp", None, "space", None, None), P("space", "dp", None)),
        check_vma=False,
    )
```

time: 204 us -> 118 us (0.58); the launches traced: 201 us -> 117 us
  local copies, waits for them, and re-layouts: 45.8 us -> 5.04 us
  matrix products: 35 us -> 0 us
  waiting for transfers between devices: 59 us -> 24.2 us
  blocking collectives: 0 us -> 30.9 us
  other arithmetic: 23.7 us -> 0 us
  Pallas kernels: 0 us -> 22.9 us
  between operations: 14.5 us -> 0.74 us
  starting transfers between devices: 22.6 us -> 33.2 us
    dot_general x18 -> x0, matrix products: 35 us -> none  [product(): jnp.einsum(equation, left_op, right_op, preferred_element_type=jnp.float32)]
    reduce_scatter x1 -> x0, waiting for transfers between devices: 28.6 us -> none  [body(): lax.psum_scatter(grad_terms.reshape(local_modes, KX, 2 * channels * chann...]
    all_to_all x0 -> x2, blocking collectives: none -> 26 us  [exchange(): return lax.all_to_all(value, axis, split_axis=0, concat_axis=0, tiled=True)]
    another operation x7 -> x0, other arithmetic: 23.1 us -> none
    pallas_call x0 -> x8, Pallas kernels: none -> 22.9 us  [run(): pl.pallas_call(kernel, out_shape=shapes, in_specs=[pl.BlockSpec(memory_sp...]
    mul x4 -> x0, local copies, waits for them, and re-layouts: 14.8 us -> none  [the longest x2 8.29 us: plane_table(): -factor * jnp.sin(angles)]
    all_to_all x4, starting transfers between devices: 22.5 us -> 33.2 us  [the longest x3 22.4 us: exchange(): return lax.all_to_all(value, axis, split_axis=0, concat_axis=0, tiled=True)]
    convert_element_type x6 -> x0, local copies, waits for them, and re-layouts: 10 us -> none  [the longest x1 6.82 us: body(): grad_terms.reshape(local_modes, KX, 2 * channels * channels)]
  transfers between devices with their start and end apart: 6 -> 4, of which waited for: 5 -> 4; matrix products, arithmetic and copies ran while one was open for 32% -> 0% of each run, Pallas kernels for 0% -> 9%
where the time goes in v1:
time: 118 us; the launch traced here: 117 us
  starting transfers between devices  33.2 us (28%)
  blocking collectives  30.9 us (26%)
  waiting for transfers between devices  24.2 us (21%)
  Pallas kernels  22.9 us (19%)
  local copies, waits for them, and re-layouts  5.04 us (4%)
    all_to_all x2, blocking collectives, exchange(): return lax.all_to_all(value, axis, split_axis=0, concat_axis=0, tiled=True)  26 us
    pallas_call x8, Pallas kernels, run(): pl.pallas_call(kernel, out_shape=shapes, in_specs=[pl.BlockSpec(memory_sp...  22.9 us
    all_to_all x3, starting transfers between devices, exchange(): return lax.all_to_all(value, axis, split_axis=0, concat_axis=0, tiled=True)  22.4 us
    all_to_all x3, waiting for transfers between devices, exchange(): return lax.all_to_all(value, axis, split_axis=0, concat_axis=0, tiled=True)  12.7 us
    all_to_all x1, waiting for transfers between devices, body(): lax.all_to_all(copies, 'dp', 0, 0, tiled=True, axis_index_groups=same_core)  11.5 us
    all_to_all x1, starting transfers between devices, body(): lax.all_to_all(copies, 'dp', 0, 0, tiled=True, axis_index_groups=same_core)  10.9 us
    unnamed x18, local copies, waits for them, and re-layouts  4.92 us
    all_gather x2, blocking collectives, body(): lax.all_gather(blocks[4 * h:4 * h + 4], 'dp', axis=0, tiled=True, axis_in...  4.88 us
  transfers between devices with their start and end apart: 4, of which 4 were waited for; matrix products, arithmetic and copies ran while one was open for 0% of the time, Pallas kernels for 9%

profile of v1, /device:TPU:1, one launch (start us, length us, event | category | flops | bytes accessed | tf_op | source)
XLA Modules:
  0.0 117.0 jit_solution(3558540369124198794)
XLA Ops:
  0.6 0.0 copy-start.4
  0.6 0.8 copy-done.4
  1.5 0.9 repeat.1
  2.3 10.9 %all-to-all-start = ((bf16[8,16,2048]{2,1,0:T(8,128)(2,1)}), bf16[8,16,2048]{2,1,0:T(8,128)(2,1)S(1)}, u32[]{:S(2)}, u32[]{:S(2)}) async-start(bf16[8,16,2048]{2,1,0:T(8,128)(2,1)} %repeat.1), calls=%async_computation | async-start | bytes 1048576 | tf_op jit(solution)/shard_map/all_to_all | solution.py:367
  13.2 0.0 copy-start
  13.2 1.6 %copy-done = bf16[512,2176]{1,0:T(8,128)(2,1)S(1)} copy-done((bf16[512,2176]{1,0:T(8,128)(2,1)S(1)}, bf16[512,2176]{1,0:T(8,128)(2,1)}, u32[]{:S(2)}) %copy-start) | copy-done | bytes 2228248
  14.8 0.0 copy-start.7
  14.8 1.2 %copy-done.7 = bf16[1,32,4,32,128]{4,3,2,1,0:T(8,128)(2,1)S(1)} copy-done((bf16[1,32,4,32,128]{4,3,2,1,0:T(8,128)(2,1)S(1)}, bf16[1,32,4,32,128]{4,3,2,1,0:T(8,128)(2,1)}, u32[]{:S(2)}) %copy-start.7) | copy-done | bytes 1048600
  16.0 3.6 %analyse.1 = (bf16[32,16,128]{2,1,0:T(8,128)(2,1)}, bf16[256,2048]{1,0:T(8,128)(2,1)}) custom-call(bf16[4096,128]{1,0:T(8,128)(2,1)S(1)} %bitcast.10, bf16[512,2176]{1,0:T(8,128)(2,1)S(1)} %copy-done), custom_call_target="tpu_custom_call" | custom-call | flops 1000000000 | bytes 2097152 | tf_op jit(solution)/shard_map/analyse/pallas_call | solution.py:335
  19.6 0.0 copy-start.3
  19.6 11.5 %all-to-all-done = bf16[8,16,2048]{2,1,0:T(8,128)(2,1)S(1)} async-done(((bf16[8,16,2048]{2,1,0:T(8,128)(2,1)}), bf16[8,16,2048]{2,1,0:T(8,128)(2,1)S(1)}, u32[]{:S(2)}, u32[]{:S(2)}) %all-to-all-start) | async-done | bytes 524320 | tf_op jit(solution)/shard_map/all_to_all | solution.py:367
  31.1 9.7 %all-to-all-start.1 = ((bf16[32,16,128]{2,1,0:T(8,128)(2,1)}), bf16[32,16,128]{2,1,0:T(8,128)(2,1)S(1)}, u32[]{:S(2)}, u32[]{:S(2)}) async-start(bf16[32,16,128]{2,1,0:T(8,128)(2,1)} %get-tuple-element.15), calls=%async_computation.1 | async-start | bytes 262144 | tf_op jit(solution)/shard_map/all_to_all | solution.py:352
  40.9 2.6 %all_gather.7 = bf16[8,16,2048]{2,1,0:T(8,128)(2,1)S(1)} all-gather(bf16[4,16,2048]{2,1,0:T(8,128)(2,1)S(1)} %get-tuple-element.26), channel_id=1, replica_groups={{0,32},{64,96},{128,160},{192,224},{256,288},{320,352},{384,416},{448,4..., dimensions={0}, use_global_device_ids=true | all-gather | bytes 786432 | tf_op jit(solution)/shard_map/all_gather | solution.py:374
  43.5 0.0 copy-start.8
  43.5 0.0 copy-start.1
  43.5 0.0 copy-start.6
  43.5 2.3 %all_gather.6 = bf16[8,16,2048]{2,1,0:T(8,128)(2,1)S(1)} all-gather(bf16[4,16,2048]{2,1,0:T(8,128)(2,1)S(1)} %get-tuple-element.27), channel_id=1, replica_groups={{0,32},{64,96},{128,160},{192,224},{256,288},{320,352},{384,416},{448,4..., dimensions={0}, use_global_device_ids=true | all-gather | bytes 786432 | tf_op jit(solution)/shard_map/all_gather | solution.py:374
  45.8 4.2 %all-to-all-done.1.recv_ref = bf16[32,16,128]{2,1,0:T(8,128)(2,1)S(1)} async-done(((bf16[32,16,128]{2,1,0:T(8,128)(2,1)}), bf16[32,16,128]{2,1,0:T(8,128)(2,1)S(1)}, u32[]{:S(2)}, u32[]{:S(2)}) %all-to-all-start.1) | async-done | bytes 131104 | tf_op jit(solution)/shard_map/all_to_all | solution.py:352
  50.0 0.0 copy-done.3
  50.0 2.3 %mix.1 = (bf16[32,16,128]{2,1,0:T(8,128)(2,1)}, f32[128,128]{1,0:T(8,128)}) custom-call(bf16[32,16,128]{2,1,0:T(8,128)(2,1)S(1)} %all-to-all-done.1.recv_ref, bf16[128,2048]{1,0:T(8,128)(2,1)S(1)} %bitcast.7, bf16[128,2048]{1,0:T(8,128)(2,1)S(1)} %bitcast.5, bf16[128,512]{1,0:T(8,128)(2,1)S(1)} %copy-done.3), custom_call_target="tpu_custom_call" | custom-call | flops 100000000 | bytes 2097152 | tf_op jit(solution)/shard_map/mix/pallas_call | solution.py:335
  52.3 5.3 %all-to-all-start.2 = ((bf16[32,16,128]{2,1,0:T(8,128)(2,1)}), bf16[32,16,128]{2,1,0:T(8,128)(2,1)S(1)}, u32[]{:S(2)}, u32[]{:S(2)}) async-start(bf16[32,16,128]{2,1,0:T(8,128)(2,1)} %get-tuple-element.17), calls=%async_computation.2 | async-start | bytes 262144 | tf_op jit(solution)/shard_map/all_to_all | solution.py:352
  57.6 0.0 copy-start.2
  57.6 1.2 %copy-done.2 = bf16[1,32,4,32,128]{4,3,2,1,0:T(8,128)(2,1)S(1)} copy-done((bf16[1,32,4,32,128]{4,3,2,1,0:T(8,128)(2,1)S(1)}, bf16[1,32,4,32,128]{4,3,2,1,0:T(8,128)(2,1)}, u32[]{:S(2)}) %copy-start.2) | copy-done | bytes 1048600
  58.9 2.8 %regroup.1.c_hbm = bf16[256,2048]{1,0:T(8,128)(2,1)} custom-call(bf16[4096,128]{1,0:T(8,128)(2,1)S(1)} %bitcast.9), custom_call_target="tpu_custom_call" | custom-call | flops 1000000 | bytes 2097152 | tf_op jit(solution)/shard_map/regroup/pallas_call | solution.py:335
  61.6 5.1 %all-to-all-done.2.recv_ref = bf16[32,16,128]{2,1,0:T(8,128)(2,1)S(1)} async-done(((bf16[32,16,128]{2,1,0:T(8,128)(2,1)}), bf16[32,16,128]{2,1,0:T(8,128)(2,1)S(1)}, u32[]{:S(2)}, u32[]{:S(2)}) %all-to-all-start.2) | async-done | bytes 131104 | tf_op jit(solution)/shard_map/all_to_all | solution.py:352
  66.8 0.0 copy-done.8
  66.8 0.1 broadcast_in_dim.2.bias_ref
  66.9 0.0 copy-done.1
  66.9 0.0 copy-done.6
  66.9 0.0 copy-start.5
  66.9 5.3 %nonlinear.1 = (bf16[32,16,128]{2,1,0:T(8,128)(2,1)S(1)}, bf16[256,2048]{1,0:T(8,128)(2,1)}) custom-call(bf16[32,16,128]{2,1,0:T(8,128)(2,1)S(1)} %all-to-all-done.2.recv_ref, bf16[512,2176]{1,0:T(8,128)(2,1)S(1)} %copy-done.1, bf16[256,2048]{1,0:T(8,128)(2,1)} %get-tuple-element.18.x_hbm, bf16[256,2048]{1,0:T(8,128)(2,1)} %regroup.1.c_hbm, ...), custom_call_target="tpu_custom_call" | custom-call | flops 2000000000 | bytes 2097152 | tf_op jit(solution)/shard_map/nonlinear/pallas_call | solution.py:335
  72.2 13.3 %all_to_all.30.recv_ref = bf16[32,16,128]{2,1,0:T(8,128)(2,1)S(1)} all-to-all(bf16[32,16,128]{2,1,0:T(8,128)(2,1)S(1)} %get-tuple-element.19), channel_id=1, replica_groups=mesh['dp'=16,'space'=32] {'space'}, dimensions={0} | all-to-all | bytes 262144 | tf_op jit(solution)/shard_map/all_to_all | solution.py:352
  85.6 0.0 copy-done.5
  85.6 1.8 %pull.1 = (bf16[32,16,128]{2,1,0:T(8,128)(2,1)S(1)}, bf16[16,16,128]{2,1,0:T(8,128)(2,1)}) custom-call(bf16[32,16,128]{2,1,0:T(8,128)(2,1)S(1)} %all_to_all.30.recv_ref, bf16[128,2048]{1,0:T(8,128)(2,1)S(1)} %bitcast.8, bf16[128,2048]{1,0:T(8,128)(2,1)S(1)} %bitcast.6, bf16[128,512]{1,0:T(8,128)(2,1)S(1)} %copy-done.3, f32[128,128]{1,0:T(8,128)S(1)} %copy-done.5), custom_call_target="tpu_custom_call" | custom-call | flops 100000000 | bytes 2097152 | tf_op jit(solution)/shard_map/pull/pallas_call | solution.py:335
  87.4 12.7 %all_to_all.31.recv_ref = bf16[32,16,128]{2,1,0:T(8,128)(2,1)S(1)} all-to-all(bf16[32,16,128]{2,1,0:T(8,128)(2,1)S(1)} %get-tuple-element.22), channel_id=1, replica_groups=mesh['dp'=16,'space'=32] {'space'}, dimensions={0} | all-to-all | bytes 262144 | tf_op jit(solution)/shard_map/all_to_all | solution.py:352
  100.1 7.4 %all-to-all-start.5 = ((bf16[16,16,128]{2,1,0:T(8,128)(2,1)}), bf16[16,16,128]{2,1,0:T(8,128)(2,1)S(1)}, u32[]{:S(2)}, u32[]{:S(2)}) async-start(bf16[16,16,128]{2,1,0:T(8,128)(2,1)} %get-tuple-element.25), calls=%async_computation.5 | async-start | bytes 131072 | tf_op jit(solution)/shard_map/all_to_all | solution.py:352
  107.5 4.5 %input_grad.1 = bf16[4096,128]{1,0:T(8,128)(2,1)} custom-call(bf16[32,16,128]{2,1,0:T(8,128)(2,1)S(1)} %all_to_all.31.recv_ref, bf16[512,2176]{1,0:T(8,128)(2,1)S(1)} %copy-done.1, bf16[256,2048]{1,0:T(8,128)(2,1)} %get-tuple-element.24.delta_hbm, bf16[32,32]{1,0:T(8,128)(2,1)S(1)} %copy-done.6), custom_call_target="tpu_custom_call" | custom-call | flops 1000000000 | bytes 2097152 | tf_op jit(solution)/shard_map/input_grad/pallas_call | solution.py:335
  112.0 3.3 %all-to-all-done.5.pair_ref = bf16[16,16,128]{2,1,0:T(8,128)(2,1)S(1)} async-done(((bf16[16,16,128]{2,1,0:T(8,128)(2,1)}), bf16[16,16,128]{2,1,0:T(8,128)(2,1)S(1)}, u32[]{:S(2)}, u32[]{:S(2)}) %all-to-all-start.5) | async-done | bytes 65568 | tf_op jit(solution)/shard_map/all_to_all | solution.py:352
  115.3 1.7 %weight_grad.1 = f32[8,2,2048]{2,1,0:T(2,128)} custom-call(bf16[16,16,128]{2,1,0:T(8,128)(2,1)S(1)} %all-to-all-done.5.pair_ref), custom_call_target="tpu_custom_call" | custom-call | flops 100000000 | bytes 2097152 | tf_op jit(solution)/shard_map/weight_grad/pallas_call | solution.py:335
  (1 shorter events, 0.0 us)
Async XLA Ops:
  0.6 0.8 copy-start.4
  2.3 28.8 %all-to-all-start = ((bf16[8,16,2048]{2,1,0:T(8,128)(2,1)}), bf16[8,16,2048]{2,1,0:T(8,128)(2,1)S(1)}, u32[]{:S(2)}, u32[]{:S(2)}) async-start(bf16[8,16,2048]{2,1,0:T(8,128)(2,1)} %repeat.1), calls=%async_computation | async-start | bytes 1048576 | tf_op jit(solution)/shard_map/all_to_all | solution.py:367
  13.2 1.6 %copy-start = (bf16[512,2176]{1,0:T(8,128)(2,1)S(1)}, bf16[512,2176]{1,0:T(8,128)(2,1)}, u32[]{:S(2)}) copy-start(bf16[512,2176]{1,0:T(8,128)(2,1)} %constant.4.clone.table_ref) | copy-start | bytes 6684676
  14.8 1.2 %copy-start.7 = (bf16[1,32,4,32,128]{4,3,2,1,0:T(8,128)(2,1)S(1)}, bf16[1,32,4,32,128]{4,3,2,1,0:T(8,128)(2,1)}, u32[]{:S(2)}) copy-start(bf16[1,32,4,32,128]{4,3,2,1,0:T(8,128)(2,1)} %param.7) | copy-start | bytes 3145732
  19.6 30.4 %copy-start.3 = (bf16[128,512]{1,0:T(8,128)(2,1)S(1)}, bf16[128,512]{1,0:T(8,128)(2,1)}, u32[]{:S(2)}) copy-start(bf16[128,512]{1,0:T(8,128)(2,1)} %constant.5.clone.line_ref) | copy-start | bytes 393220
  31.1 18.8 %all-to-all-start.1 = ((bf16[32,16,128]{2,1,0:T(8,128)(2,1)}), bf16[32,16,128]{2,1,0:T(8,128)(2,1)S(1)}, u32[]{:S(2)}, u32[]{:S(2)}) async-start(bf16[32,16,128]{2,1,0:T(8,128)(2,1)} %get-tuple-element.15), calls=%async_computation.1 | async-start | bytes 262144 | tf_op jit(solution)/shard_map/all_to_all | solution.py:352
  43.5 23.3 %copy-start.8 = (bf16[32]{0:T(256)(128)(2,1)S(1)}, bf16[32]{0:T(256)(128)(2,1)}, u32[]{:S(2)}) copy-start(bf16[32]{0:T(256)(128)(2,1)} %param.11) | copy-start | bytes 196
  43.5 23.4 %copy-start.1 = (bf16[512,2176]{1,0:T(8,128)(2,1)S(1)}, bf16[512,2176]{1,0:T(8,128)(2,1)}, u32[]{:S(2)}) copy-start(bf16[512,2176]{1,0:T(8,128)(2,1)} %constant.4.clone.table_ref) | copy-start | bytes 6684676
  43.5 23.4 %copy-start.6 = (bf16[32,32]{1,0:T(8,128)(2,1)S(1)}, bf16[32,32]{1,0:T(8,128)(2,1)}, u32[]{:S(2)}) copy-start(bf16[32,32]{1,0:T(8,128)(2,1)} %weights_ref.3) | copy-start | bytes 6148
  52.3 14.4 %all-to-all-start.2 = ((bf16[32,16,128]{2,1,0:T(8,128)(2,1)}), bf16[32,16,128]{2,1,0:T(8,128)(2,1)S(1)}, u32[]{:S(2)}, u32[]{:S(2)}) async-start(bf16[32,16,128]{2,1,0:T(8,128)(2,1)} %get-tuple-element.17), calls=%async_computation.2 | async-start | bytes 262144 | tf_op jit(solution)/shard_map/all_to_all | solution.py:352
  57.6 1.2 %copy-start.2 = (bf16[1,32,4,32,128]{4,3,2,1,0:T(8,128)(2,1)S(1)}, bf16[1,32,4,32,128]{4,3,2,1,0:T(8,128)(2,1)}, u32[]{:S(2)}) copy-start(bf16[1,32,4,32,128]{4,3,2,1,0:T(8,128)(2,1)} %param.8) | copy-start | bytes 3145732
  66.9 18.7 %copy-start.5 = (f32[128,128]{1,0:T(8,128)S(1)}, f32[128,128]{1,0:T(8,128)}, u32[]{:S(2)}) copy-start(f32[128,128]{1,0:T(8,128)} %get-tuple-element.20.spec_ref) | copy-start | bytes 196612
  100.1 15.2 %all-to-all-start.5 = ((bf16[16,16,128]{2,1,0:T(8,128)(2,1)}), bf16[16,16,128]{2,1,0:T(8,128)(2,1)S(1)}, u32[]{:S(2)}, u32[]{:S(2)}) async-start(bf16[16,16,128]{2,1,0:T(8,128)(2,1)} %get-tuple-element.25), calls=%async_computation.5 | async-start | bytes 131072 | tf_op jit(solution)/shard_map/all_to_all | solution.py:352

commit v2 on v1

--- a/solution.py
+++ b/solution.py
@@ -64,11 +64,9 @@
 
 
 def gelu_slope(values):
-    inner_arg = tanh_coef * (values + cubic_coef * values * values * values)
-    tanh_part = jnp.tanh(inner_arg)
-    return 0.5 * (1.0 + tanh_part) + 0.5 * values * (1.0 - tanh_part * tanh_part) * tanh_coef * (
-        1.0 + 3.0 * cubic_coef * values * values
-    )
+    square = values * values
+    half = 0.5 + 0.5 * jnp.tanh(values * (tanh_coef + (tanh_coef * cubic_coef) * square))
+    return half + (half - half * half) * (values * (2.0 * tanh_coef + (6.0 * tanh_coef * cubic_coef) * square))
 
 
 def dot(left, right, dims=((1,), (0,))):
@@ -152,10 +150,13 @@
     return ((row >> 7) & 1) * 8 + ((row >> 4) & 3) * 2 + ((row >> 6) & 1)
 
 
-def repeat_kernel(spectral_ref, out_ref):
-    rows = jnp.concatenate([spectral_ref[m].astype(F32) for m in range(8)], axis=0).astype(BF16)
-    for z in range(8):
-        out_ref[z] = rows
+def repeat_kernel(spectral_ref, out_hbm, rows_ref, sems):
+    rows_ref[...] = jnp.concatenate([spectral_ref[m].astype(F32) for m in range(8)], axis=0).astype(BF16)
+    copies = [pltpu.make_async_copy(rows_ref, out_hbm.at[z], sems.at[z]) for z in range(8)]
+    for copy in copies:
+        copy.start()
+    for copy in copies:
+        copy.wait()
 
 
 def weight_columns(low_ref, high_ref, start):
@@ -180,10 +181,10 @@
     return dot(select, kept).astype(BF16)
 
 
-def mix_kernel(recv_ref, low_ref, high_ref, line_ref, send_out, spec_out, send_ref, spec_ref, sems):
+def mix_kernel(recv_ref, low_ref, high_ref, line_ref, send_ref, spec_out, spec_ref, sem):
     compact = dot(line_ref[...], recv_ref[...].reshape(512, 128)).astype(BF16)
     spec_ref[...] = compact.astype(F32)
-    spec_copy = pltpu.make_async_copy(spec_ref, spec_out, sems.at[0])
+    spec_copy = pltpu.make_async_copy(spec_ref, spec_out, sem)
     spec_copy.start()
     rows = spread_rows(compact)
     out_real = jnp.zeros((256, 128), F32)
@@ -201,10 +202,7 @@
     mixed = mixed + pltpu.roll(mixed, 64, 1)
     compact = close_rows(mixed)
     send_ref[...] = dot(line_ref[...], compact, ((0,), (0,))).astype(BF16).reshape(32, 16, 128)
-    send_copy = pltpu.make_async_copy(send_ref, send_out, sems.at[1])
-    send_copy.start()
     spec_copy.wait()
-    send_copy.wait()
 
 
 def pull_kernel(recv_ref, low_ref, high_ref, line_ref, spec_ref, send_ref, pair_ref):
@@ -250,51 +248,66 @@
     return both.T.astype(BF16)
 
 
+def quarters(source, target, sems):
+    width = 4 * NZ
+    return [
+        pltpu.make_async_copy(
+            source.at[:, pl.ds(q * width, width)], target.at[:, pl.ds(q * width, width)], sems.at[q]
+        )
+        for q in range(4)
+    ]
+
+
 def step_lanes():
     return [(2 * t * NZ, 2 * NZ) for t in range(7)] + [(14 * NZ, NZ)]
 
 
 def nonlinear_kernel(
-    recv_ref, table_ref, x_hbm, c_hbm, weights_ref, bias_ref, send_ref, delta_out, x_ref, c_ref, delta_ref, sems
+    recv_ref, table_ref, x_hbm, c_hbm, weights_ref, bias_ref, send_ref, delta_out, x_ref, c_ref, delta_ref, spec_ref, sems
 ):
-    x_copy = pltpu.make_async_copy(x_hbm, x_ref, sems.at[0])
-    x_copy.start()
-    c_copy = pltpu.make_async_copy(c_hbm, c_ref, sems.at[1])
-    c_copy.start()
+    x_copies = quarters(x_hbm, x_ref, sems.at[0])
+    c_copies = quarters(c_hbm, c_ref, sems.at[1])
+    out_copies = quarters(delta_ref, delta_out, sems.at[2])
+    for q in range(4):
+        x_copies[q].start()
+        c_copies[q].start()
     basis = profiles(recv_ref, True)
     mixing, spread = block_weights(weights_ref, True)
     bias = dot(spread, bias_ref[...])
-    x_copy.wait()
-    c_copy.wait()
+    last = slice(STEPS * NZ, 16 * NZ)
     for start, width in step_lanes():
         lanes = slice(start, start + width)
-        pre = dot(basis, table_ref[:, lanes]) + dot(mixing, x_ref[:, lanes]) + bias[:, 0:width]
-        delta_ref[:, lanes] = (c_ref[:, lanes].astype(F32) * gelu_slope(pre)).astype(BF16)
-    last = slice(STEPS * NZ, 16 * NZ)
-    alone = jnp.concatenate(
-        [dot(basis[0:128], table_ref[:, last]), dot(basis[0:128], table_ref[:, 16 * NZ : 17 * NZ])], axis=0
-    )
-    pre = alone + dot(mixing, x_ref[:, last]) + bias[:, 0:NZ]
-    delta_ref[:, last] = (c_ref[:, last].astype(F32) * gelu_slope(pre)).astype(BF16)
-    copy = pltpu.make_async_copy(delta_ref, delta_out, sems.at[2])
-    copy.start()
+        spec_ref[:, lanes] = dot(basis, table_ref[:, lanes]) + bias[:, 0:width]
+    spec_ref[0:128, last] = dot(basis[0:128], table_ref[:, last]) + bias[0:128, 0:NZ]
+    spec_ref[128:256, last] = dot(basis[0:128], table_ref[:, 16 * NZ : 17 * NZ]) + bias[128:256, 0:NZ]
+    for q in range(4):
+        x_copies[q].wait()
+        c_copies[q].wait()
+        for t in range(2):
+            lanes = pl.ds((4 * q + 2 * t) * NZ, 2 * NZ)
+            pre = spec_ref[:, lanes] + dot(mixing, x_ref[:, lanes])
+            delta_ref[:, lanes] = (c_ref[:, lanes].astype(F32) * gelu_slope(pre)).astype(BF16)
+        out_copies[q].start()
     coarse = doubled(to_coarse(table_ref, delta_ref))
     send_ref[...] = swap_blocks(coarse).astype(BF16).reshape(32, 16, 128)
-    copy.wait()
-
-
-def input_grad_kernel(recv_ref, table_ref, delta_hbm, weights_ref, out_ref, wide, delta_ref, sem):
-    copy = pltpu.make_async_copy(delta_hbm, delta_ref, sem)
-    copy.start()
+    for copy in out_copies:
+        copy.wait()
+
+
+def input_grad_kernel(recv_ref, table_ref, delta_hbm, weights_ref, out_hbm, wide, delta_ref, out_ref, sems):
+    copies = quarters(delta_hbm, delta_ref, sems.at[0])
+    for copy in copies:
+        copy.start()
     basis = profiles(recv_ref, False)
     mixing, _ = block_weights(weights_ref, False)
-    copy.wait()
 
     def put(value, y):
         for x in range(SLAB):
             wide[pl.ds(x * NY + y, C, stride=SLAB * NY), :] = value[x * C : x * C + C]
 
-    for start, width in step_lanes():
+    for t, (start, width) in enumerate(step_lanes()):
+        if t % 2 == 0:
+            copies[t // 2].wait()
         lanes = slice(start, start + width)
         grad = dot(basis, table_ref[:, lanes]) + dot(mixing, delta_ref[:, lanes])
         for u in range(width // NZ):
@@ -305,7 +318,15 @@
     linear = dot(mixing, delta_ref[:, last])
     put(dot(basis[0:128], table_ref[:, last]) + linear[0:128], 0)
     put(dot(basis[0:128], table_ref[:, 16 * NZ : 17 * NZ]) + linear[128:256], 16)
-    out_ref[...] = wide[...].astype(BF16)
+    size = C * SLAB * NY // 4
+    copies = []
+    for q in range(4):
+        rows = pl.ds(q * size, size)
+        out_ref[rows, :] = wide[rows, :].astype(BF16)
+        copies.append(pltpu.make_async_copy(out_ref.at[rows, :], out_hbm.at[rows, :], sems.at[1, q]))
+        copies[q].start()
+    for copy in copies:
+        copy.wait()
 
 
 def weight_grad_kernel(pair_ref, out_ref):
@@ -363,29 +384,31 @@
 
     same_core = [[2 * z + core for z in range(8)] for core in range(2)]
     same_chip = [[2 * z, 2 * z + 1] for z in range(8)]
-    (copies,) = run(repeat_kernel, "repeat", [((8, 16, 2048), BF16)], [spectral], 10**6)
+    (copies,) = run(repeat_kernel, "repeat", [((8, 16, 2048), BF16)], [spectral], 10**6,
+        [pltpu.VMEM((16, 2048), BF16), pltpu.SemaphoreType.DMA((8,))], (0,),
+    )
     blocks = lax.all_to_all(copies, "dp", 0, 0, tiled=True, axis_index_groups=same_core)
     send, x_pairs = run(
         analyse_kernel, "analyse", [piece, pairs], [features.reshape(C * SLAB * NY, NZ), table], 10**9,
         [wide, held, sem], (1,),
     )
-    send, blocks = lax.optimization_barrier((send, blocks))
+    (c_pairs,) = run(
+        regroup_kernel, "regroup", [pairs], [cotangent.reshape(C * SLAB * NY, NZ)], 10**6, [wide, held, sem], (0,)
+    )
+    send, blocks, c_pairs = lax.optimization_barrier((send, blocks, c_pairs))
     w_low, w_high = (
         lax.all_gather(blocks[4 * h : 4 * h + 4], "dp", axis=0, tiled=True, axis_index_groups=same_chip).reshape(128, 2048)
         for h in range(2)
     )
-    (c_pairs,) = run(
-        regroup_kernel, "regroup", [pairs], [cotangent.reshape(C * SLAB * NY, NZ)], 10**6, [wide, held, sem], (0,)
-    )
     send, spec = run(
         mix_kernel, "mix", [piece, ((128, 128), F32)], [exchange(send, "space"), w_low, w_high, line], 10**8,
-        [pltpu.VMEM(*piece), pltpu.VMEM((128, 128), F32), pltpu.SemaphoreType.DMA((2,))], (0, 1),
+        [pltpu.VMEM((128, 128), F32), sem], (1,),
     )
     bias = jnp.broadcast_to(biases[:, None], (C, 2 * NZ))
     send, delta = run(
         nonlinear_kernel, "nonlinear", [piece, pairs],
         [exchange(send, "space"), table, x_pairs, c_pairs, pointwise, bias], 2 * 10**9,
-        [held, held, held, pltpu.SemaphoreType.DMA((3,))], (1,), (2, 3),
+        [held, held, held, pltpu.VMEM((256, 16 * NZ), F32), pltpu.SemaphoreType.DMA((3, 4))], (1,), (2, 3),
     )
     send, pair = run(
         pull_kernel, "pull", [piece, ((16, 16, 128), BF16)],
@@ -396,7 +419,8 @@
     pair = exchange(pair, "dp")
     (grad_input,) = run(
         input_grad_kernel, "input_grad", [((C * SLAB * NY, NZ), BF16)],
-        [recv, table, delta, pointwise], 10**9, [wide, held, sem], (), (2,),
+        [recv, table, delta, pointwise], 10**9,
+        [wide, held, pltpu.VMEM((C * SLAB * NY, NZ), BF16), pltpu.SemaphoreType.DMA((2, 4))], (0,), (2,),
     )
     (grad_spectral,) = run(weight_grad_kernel, "weight_grad", [((8, 2, 2048), F32)], [pair], 10**8)
     return grad_input.reshape(features.shape), grad_spectral

time: 118 us -> 116 us (0.983)
  blocking collectives: 30.9 us -> 44.9 us
  waiting for transfers between devices: 24.2 us -> 16.6 us
  starting transfers between devices: 33.2 us -> 28.1 us
  local copies, waits for them, and re-layouts: 5.04 us -> 3.56 us
    all_to_all x2 -> x3, blocking collectives: 26 us -> 40.1 us  [exchange(): return lax.all_to_all(value, axis, split_axis=0, concat_axis=0, tiled=True)]
    all_to_all x3 -> x2, starting transfers between devices: 22.4 us -> 17.2 us  [exchange(): return lax.all_to_all(value, axis, split_axis=0, concat_axis=0, tiled=True)]
    all_to_all x3 -> x2, waiting for transfers between devices: 12.7 us -> 7.54 us  [exchange(): return lax.all_to_all(value, axis, split_axis=0, concat_axis=0, tiled=True)]
    all_to_all x1, waiting for transfers between devices: 11.5 us -> 9.11 us  [body(): lax.all_to_all(copies, 'dp', 0, 0, tiled=True, axis_index_groups=same_core)]
    unnamed x18 -> x16, local copies, waits for them, and re-layouts: 4.92 us -> 3.45 us
  transfers between devices with their start and end apart: 4 -> 3, of which waited for: 4 -> 3; matrix products, arithmetic and copies ran while one was open for 0% -> 0% of each run, Pallas kernels for 9% -> 10%
where the time goes in v2:
time: 116 us
  blocking collectives  44.9 us (39%)
  starting transfers between devices  28.1 us (24%)
  Pallas kernels  21.9 us (19%)
  waiting for transfers between devices  16.6 us (14%)
  local copies, waits for them, and re-layouts  3.56 us (3%)
    all_to_all x3, blocking collectives, exchange(): return lax.all_to_all(value, axis, split_axis=0, concat_axis=0, tiled=True)  40.1 us
    pallas_call x8, Pallas kernels, run(): pl.pallas_call(kernel, out_shape=shapes, in_specs=[pl.BlockSpec(memory_sp...  21.9 us
    all_to_all x2, starting transfers between devices, exchange(): return lax.all_to_all(value, axis, split_axis=0, concat_axis=0, tiled=True)  17.2 us
    all_to_all x1, starting transfers between devices, body(): lax.all_to_all(copies, 'dp', 0, 0, tiled=True, axis_index_groups=same_core)  10.9 us
    all_to_all x1, waiting for transfers between devices, body(): lax.all_to_all(copies, 'dp', 0, 0, tiled=True, axis_index_groups=same_core)  9.11 us
    all_to_all x2, waiting for transfers between devices, exchange(): return lax.all_to_all(value, axis, split_axis=0, concat_axis=0, tiled=True)  7.54 us
    all_gather x2, blocking collectives, body(): lax.all_gather(blocks[4 * h:4 * h + 4], 'dp', axis=0, tiled=True, axis_in...  4.75 us
    unnamed x16, local copies, waits for them, and re-layouts  3.45 us
  transfers between devices with their start and end apart: 3, of which 3 were waited for; matrix products, arithmetic and copies ran while one was open for 0% of the time, Pallas kernels for 10%

profile of v2, /device:TPU:1, one launch (start us, length us, event | category | flops | bytes accessed | tf_op | source)
XLA Modules:
  0.0 115.8 jit_solution(4040638290513033463)
XLA Ops:
  0.6 0.0 copy-start
  0.6 0.0 copy-start.3
  0.7 1.0 copy-done.3
  1.6 0.9 repeat.1
  2.6 10.9 %all-to-all-start = ((bf16[8,16,2048]{2,1,0:T(8,128)(2,1)}), bf16[8,16,2048]{2,1,0:T(8,128)(2,1)S(1)}, u32[]{:S(2)}, u32[]{:S(2)}) async-start(bf16[8,16,2048]{2,1,0:T(8,128)(2,1)} %repeat.1), calls=%async_computation | async-start | bytes 1048576 | tf_op jit(solution)/shard_map/all_to_all | solution.py:390
  13.5 0.0 copy-start.1
  13.5 1.2 %copy-done.1 = bf16[1,32,4,32,128]{4,3,2,1,0:T(8,128)(2,1)S(1)} copy-done((bf16[1,32,4,32,128]{4,3,2,1,0:T(8,128)(2,1)S(1)}, bf16[1,32,4,32,128]{4,3,2,1,0:T(8,128)(2,1)}, u32[]{:S(2)}) %copy-start.1) | copy-done | bytes 1048600
  14.7 2.8 %regroup.1.c_hbm = bf16[256,2048]{1,0:T(8,128)(2,1)} custom-call(bf16[4096,128]{1,0:T(8,128)(2,1)S(1)} %bitcast.9), custom_call_target="tpu_custom_call" | custom-call | flops 1000000 | bytes 2097152 | tf_op jit(solution)/shard_map/regroup/pallas_call | solution.py:356
  17.5 0.0 copy-done
  17.5 0.0 copy-start.6
  17.5 1.2 %copy-done.6 = bf16[1,32,4,32,128]{4,3,2,1,0:T(8,128)(2,1)S(1)} copy-done((bf16[1,32,4,32,128]{4,3,2,1,0:T(8,128)(2,1)S(1)}, bf16[1,32,4,32,128]{4,3,2,1,0:T(8,128)(2,1)}, u32[]{:S(2)}) %copy-start.6) | copy-done | bytes 1048600
  18.7 3.6 %analyse.1 = (bf16[32,16,128]{2,1,0:T(8,128)(2,1)}, bf16[256,2048]{1,0:T(8,128)(2,1)}) custom-call(bf16[4096,128]{1,0:T(8,128)(2,1)S(1)} %bitcast.10, bf16[512,2176]{1,0:T(8,128)(2,1)S(1)} %copy-done), custom_call_target="tpu_custom_call" | custom-call | flops 1000000000 | bytes 2097152 | tf_op jit(solution)/shard_map/analyse/pallas_call | solution.py:356
  22.3 0.0 copy-start.2
  22.3 9.1 %all-to-all-done = bf16[8,16,2048]{2,1,0:T(8,128)(2,1)S(1)} async-done(((bf16[8,16,2048]{2,1,0:T(8,128)(2,1)}), bf16[8,16,2048]{2,1,0:T(8,128)(2,1)S(1)}, u32[]{:S(2)}, u32[]{:S(2)}) %all-to-all-start) | async-done | bytes 524320 | tf_op jit(solution)/shard_map/all_to_all | solution.py:390
  31.4 0.0 copy-start.7
  31.4 0.0 copy-start.5
  31.4 9.8 %all-to-all-start.1 = ((bf16[32,16,128]{2,1,0:T(8,128)(2,1)}), bf16[32,16,128]{2,1,0:T(8,128)(2,1)S(1)}, u32[]{:S(2)}, u32[]{:S(2)}) async-start(bf16[32,16,128]{2,1,0:T(8,128)(2,1)} %get-tuple-element.16), calls=%async_computation.1 | async-start | bytes 262144 | tf_op jit(solution)/shard_map/all_to_all | solution.py:373
  41.3 2.6 %all_gather.7 = bf16[8,16,2048]{2,1,0:T(8,128)(2,1)S(1)} all-gather(bf16[4,16,2048]{2,1,0:T(8,128)(2,1)S(1)} %get-tuple-element.28), channel_id=1, replica_groups={{0,32},{64,96},{128,160},{192,224},{256,288},{320,352},{384,416},{448,4..., dimensions={0}, use_global_device_ids=true | all-gather | bytes 786432 | tf_op jit(solution)/shard_map/all_gather | solution.py:400
  43.9 2.2 %all_gather.6 = bf16[8,16,2048]{2,1,0:T(8,128)(2,1)S(1)} all-gather(bf16[4,16,2048]{2,1,0:T(8,128)(2,1)S(1)} %get-tuple-element.29), channel_id=1, replica_groups={{0,32},{64,96},{128,160},{192,224},{256,288},{320,352},{384,416},{448,4..., dimensions={0}, use_global_device_ids=true | all-gather | bytes 786432 | tf_op jit(solution)/shard_map/all_gather | solution.py:400
  46.0 4.4 %all-to-all-done.1.recv_ref = bf16[32,16,128]{2,1,0:T(8,128)(2,1)S(1)} async-done(((bf16[32,16,128]{2,1,0:T(8,128)(2,1)}), bf16[32,16,128]{2,1,0:T(8,128)(2,1)S(1)}, u32[]{:S(2)}, u32[]{:S(2)}) %all-to-all-start.1) | async-done | bytes 131104 | tf_op jit(solution)/shard_map/all_to_all | solution.py:373
  50.4 0.0 copy-done.2
  50.4 2.0 %mix.1 = (bf16[32,16,128]{2,1,0:T(8,128)(2,1)S(1)}, f32[128,128]{1,0:T(8,128)}) custom-call(bf16[32,16,128]{2,1,0:T(8,128)(2,1)S(1)} %all-to-all-done.1.recv_ref, bf16[128,2048]{1,0:T(8,128)(2,1)S(1)} %bitcast.7, bf16[128,2048]{1,0:T(8,128)(2,1)S(1)} %bitcast.5, bf16[128,512]{1,0:T(8,128)(2,1)S(1)} %copy-done.2), custom_call_target="tpu_custom_call" | custom-call | flops 100000000 | bytes 2097152 | tf_op jit(solution)/shard_map/mix/pallas_call | solution.py:356
  52.4 14.1 %all_to_all.30.recv_ref = bf16[32,16,128]{2,1,0:T(8,128)(2,1)S(1)} all-to-all(bf16[32,16,128]{2,1,0:T(8,128)(2,1)S(1)} %get-tuple-element.18), channel_id=1, replica_groups=mesh['dp'=16,'space'=32] {'space'}, dimensions={0} | all-to-all | bytes 262144 | tf_op jit(solution)/shard_map/all_to_all | solution.py:373
  66.5 0.0 copy-done.7
  66.5 0.1 broadcast_in_dim.2.bias_ref
  66.6 0.0 copy-done.5
  66.6 0.0 copy-start.4
  66.6 4.4 %nonlinear.1 = (bf16[32,16,128]{2,1,0:T(8,128)(2,1)S(1)}, bf16[256,2048]{1,0:T(8,128)(2,1)}) custom-call(bf16[32,16,128]{2,1,0:T(8,128)(2,1)S(1)} %all_to_all.30.recv_ref, bf16[512,2176]{1,0:T(8,128)(2,1)S(1)} %copy-done, bf16[256,2048]{1,0:T(8,128)(2,1)} %get-tuple-element.19.x_hbm, bf16[256,2048]{1,0:T(8,128)(2,1)} %regroup.1.c_hbm, ...), custom_call_target="tpu_custom_call" | custom-call | flops 2000000000 | bytes 2097152 | tf_op jit(solution)/shard_map/nonlinear/pallas_call | solution.py:356
  71.1 13.3 %all_to_all.31.recv_ref = bf16[32,16,128]{2,1,0:T(8,128)(2,1)S(1)} all-to-all(bf16[32,16,128]{2,1,0:T(8,128)(2,1)S(1)} %get-tuple-element.21), channel_id=1, replica_groups=mesh['dp'=16,'space'=32] {'space'}, dimensions={0} | all-to-all | bytes 262144 | tf_op jit(solution)/shard_map/all_to_all | solution.py:373
  84.4 0.0 copy-done.4
  84.4 1.8 %pull.1 = (bf16[32,16,128]{2,1,0:T(8,128)(2,1)S(1)}, bf16[16,16,128]{2,1,0:T(8,128)(2,1)}) custom-call(bf16[32,16,128]{2,1,0:T(8,128)(2,1)S(1)} %all_to_all.31.recv_ref, bf16[128,2048]{1,0:T(8,128)(2,1)S(1)} %bitcast.8, bf16[128,2048]{1,0:T(8,128)(2,1)S(1)} %bitcast.6, bf16[128,512]{1,0:T(8,128)(2,1)S(1)} %copy-done.2, f32[128,128]{1,0:T(8,128)S(1)} %copy-done.4), custom_call_target="tpu_custom_call" | custom-call | flops 100000000 | bytes 2097152 | tf_op jit(solution)/shard_map/pull/pallas_call | solution.py:356
  86.2 12.7 %all_to_all.32.recv_ref = bf16[32,16,128]{2,1,0:T(8,128)(2,1)S(1)} all-to-all(bf16[32,16,128]{2,1,0:T(8,128)(2,1)S(1)} %get-tuple-element.24), channel_id=1, replica_groups=mesh['dp'=16,'space'=32] {'space'}, dimensions={0} | all-to-all | bytes 262144 | tf_op jit(solution)/shard_map/all_to_all | solution.py:373
  98.9 7.4 %all-to-all-start.5 = ((bf16[16,16,128]{2,1,0:T(8,128)(2,1)}), bf16[16,16,128]{2,1,0:T(8,128)(2,1)S(1)}, u32[]{:S(2)}, u32[]{:S(2)}) async-start(bf16[16,16,128]{2,1,0:T(8,128)(2,1)} %get-tuple-element.27), calls=%async_computation.5 | async-start | bytes 131072 | tf_op jit(solution)/shard_map/all_to_all | solution.py:373
  106.3 4.7 %input_grad.1 = bf16[4096,128]{1,0:T(8,128)(2,1)} custom-call(bf16[32,16,128]{2,1,0:T(8,128)(2,1)S(1)} %all_to_all.32.recv_ref, bf16[512,2176]{1,0:T(8,128)(2,1)S(1)} %copy-done, bf16[256,2048]{1,0:T(8,128)(2,1)} %get-tuple-element.26.delta_hbm, bf16[32,32]{1,0:T(8,128)(2,1)S(1)} %copy-done.5), custom_call_target="tpu_custom_call" | custom-call | flops 1000000000 | bytes 2097152 | tf_op jit(solution)/shard_map/input_grad/pallas_call | solution.py:356
  111.0 3.2 %all-to-all-done.5.pair_ref = bf16[16,16,128]{2,1,0:T(8,128)(2,1)S(1)} async-done(((bf16[16,16,128]{2,1,0:T(8,128)(2,1)}), bf16[16,16,128]{2,1,0:T(8,128)(2,1)S(1)}, u32[]{:S(2)}, u32[]{:S(2)}) %all-to-all-start.5) | async-done | bytes 65568 | tf_op jit(solution)/shard_map/all_to_all | solution.py:373
  114.2 1.7 %weight_grad.1 = f32[8,2,2048]{2,1,0:T(2,128)} custom-call(bf16[16,16,128]{2,1,0:T(8,128)(2,1)S(1)} %all-to-all-done.5.pair_ref), custom_call_target="tpu_custom_call" | custom-call | flops 100000000 | bytes 2097152 | tf_op jit(solution)/shard_map/weight_grad/pallas_call | solution.py:356
  (1 shorter events, 0.0 us)
Async XLA Ops:
  0.6 16.8 %copy-start = (bf16[512,2176]{1,0:T(8,128)(2,1)S(1)}, bf16[512,2176]{1,0:T(8,128)(2,1)}, u32[]{:S(2)}) copy-start(bf16[512,2176]{1,0:T(8,128)(2,1)} %constant.4.clone.table_ref) | copy-start | bytes 6684676
  0.6 1.0 copy-start.3
  2.6 28.8 %all-to-all-start = ((bf16[8,16,2048]{2,1,0:T(8,128)(2,1)}), bf16[8,16,2048]{2,1,0:T(8,128)(2,1)S(1)}, u32[]{:S(2)}, u32[]{:S(2)}) async-start(bf16[8,16,2048]{2,1,0:T(8,128)(2,1)} %repeat.1), calls=%async_computation | async-start | bytes 1048576 | tf_op jit(solution)/shard_map/all_to_all | solution.py:390
  13.5 1.2 %copy-start.1 = (bf16[1,32,4,32,128]{4,3,2,1,0:T(8,128)(2,1)S(1)}, bf16[1,32,4,32,128]{4,3,2,1,0:T(8,128)(2,1)}, u32[]{:S(2)}) copy-start(bf16[1,32,4,32,128]{4,3,2,1,0:T(8,128)(2,1)} %param.8) | copy-start | bytes 3145732
  17.5 1.2 %copy-start.6 = (bf16[1,32,4,32,128]{4,3,2,1,0:T(8,128)(2,1)S(1)}, bf16[1,32,4,32,128]{4,3,2,1,0:T(8,128)(2,1)}, u32[]{:S(2)}) copy-start(bf16[1,32,4,32,128]{4,3,2,1,0:T(8,128)(2,1)} %param.7) | copy-start | bytes 3145732
  22.3 28.1 %copy-start.2 = (bf16[128,512]{1,0:T(8,128)(2,1)S(1)}, bf16[128,512]{1,0:T(8,128)(2,1)}, u32[]{:S(2)}) copy-start(bf16[128,512]{1,0:T(8,128)(2,1)} %constant.5.clone.line_ref) | copy-start | bytes 393220
  31.4 35.1 %copy-start.7 = (bf16[32]{0:T(256)(128)(2,1)S(1)}, bf16[32]{0:T(256)(128)(2,1)}, u32[]{:S(2)}) copy-start(bf16[32]{0:T(256)(128)(2,1)} %param.11) | copy-start | bytes 196
  31.4 35.2 %copy-start.5 = (bf16[32,32]{1,0:T(8,128)(2,1)S(1)}, bf16[32,32]{1,0:T(8,128)(2,1)}, u32[]{:S(2)}) copy-start(bf16[32,32]{1,0:T(8,128)(2,1)} %weights_ref.3) | copy-start | bytes 6148
  31.4 19.0 %all-to-all-start.1 = ((bf16[32,16,128]{2,1,0:T(8,128)(2,1)}), bf16[32,16,128]{2,1,0:T(8,128)(2,1)S(1)}, u32[]{:S(2)}, u32[]{:S(2)}) async-start(bf16[32,16,128]{2,1,0:T(8,128)(2,1)} %get-tuple-element.16), calls=%async_computation.1 | async-start | bytes 262144 | tf_op jit(solution)/shard_map/all_to_all | solution.py:373
  66.6 17.8 %copy-start.4 = (f32[128,128]{1,0:T(8,128)S(1)}, f32[128,128]{1,0:T(8,128)}, u32[]{:S(2)}) copy-start(f32[128,128]{1,0:T(8,128)} %get-tuple-element.22.spec_ref) | copy-start | bytes 196612
  98.9 15.2 %all-to-all-start.5 = ((bf16[16,16,128]{2,1,0:T(8,128)(2,1)}), bf16[16,16,128]{2,1,0:T(8,128)(2,1)S(1)}, u32[]{:S(2)}, u32[]{:S(2)}) async-start(bf16[16,16,128]{2,1,0:T(8,128)(2,1)} %get-tuple-element.27), calls=%async_computation.5 | async-start | bytes 131072 | tf_op jit(solution)/shard_map/all_to_all | solution.py:373

commit v3 on v2

--- a/solution.py
+++ b/solution.py
@@ -146,8 +146,11 @@
     copy.wait()
 
 
-def block_of(row):
-    return ((row >> 7) & 1) * 8 + ((row >> 4) & 3) * 2 + ((row >> 6) & 1)
+def spread_rows():
+    row = iota((512, 128), 0)
+    block = ((row >> 7) & 1) * 8 + ((row >> 4) & 3) * 2 + ((row >> 6) & 1)
+    wanted = block * 8 + (row >> 8) * 4 + ((row >> 3) & 1) * 2 + (row & 1)
+    return as_bf16(wanted == iota((512, 128), 1))
 
 
 def repeat_kernel(spectral_ref, out_hbm, rows_ref, sems):
@@ -164,34 +167,21 @@
     return jnp.concatenate([low_ref[:, lanes], high_ref[:, lanes]], axis=0).astype(F32)
 
 
-def spread_rows(compact):
+def own_lanes(rows):
     row = iota((512, 128), 0)
-    wanted = block_of(row) * 8 + (row >> 8) * 4 + ((row >> 3) & 1) * 2 + (row & 1)
-    select = as_bf16(wanted == iota((512, 128), 1))
-    rows = dot(select, compact)
     return jnp.where((iota((512, 128), 1) >> 5) == ((row >> 1) & 3), rows, 0.0).astype(BF16)
 
 
-def close_rows(rows):
-    row = iota((512, 128), 0)
-    kept = jnp.where((iota((512, 128), 1) >> 5) == ((row >> 1) & 3), rows, 0.0).astype(BF16)
-    col = iota((128, 512), 1)
-    wanted = block_of(col) * 8 + (col >> 8) * 4 + ((col >> 3) & 1) * 2 + (col & 1)
-    select = as_bf16(wanted == iota((128, 512), 0))
-    return dot(select, kept).astype(BF16)
-
-
-def mix_kernel(recv_ref, low_ref, high_ref, line_ref, send_ref, spec_out, spec_ref, sem):
+def mix_kernel(recv_ref, low_ref, high_ref, line_ref, send_ref, spec_ref):
     compact = dot(line_ref[...], recv_ref[...].reshape(512, 128)).astype(BF16)
     spec_ref[...] = compact.astype(F32)
-    spec_copy = pltpu.make_async_copy(spec_ref, spec_out, sem)
-    spec_copy.start()
-    rows = spread_rows(compact)
+    spread = spread_rows()
+    rows = own_lanes(dot(spread, compact))
     out_real = jnp.zeros((256, 128), F32)
     out_imag = jnp.zeros((256, 128), F32)
     for t in range(8):
-        spread = as_bf16((iota((128, 128), 0) & 31) == t * 4 + (iota((128, 128), 1) >> 5))
-        wide = dot(rows, spread)
+        repeat = as_bf16((iota((128, 128), 0) & 31) == t * 4 + (iota((128, 128), 1) >> 5))
+        wide = dot(rows, repeat)
         s_real, s_imag = wide[0:256], wide[256:512]
         w_real = weight_columns(low_ref, high_ref, t * 128)
         w_imag = weight_columns(low_ref, high_ref, 1024 + t * 128)
@@ -200,9 +190,8 @@
     mixed = jnp.concatenate([out_real, out_imag], axis=0)
     mixed = mixed + pltpu.roll(mixed, 32, 1)
     mixed = mixed + pltpu.roll(mixed, 64, 1)
-    compact = close_rows(mixed)
+    compact = dot(spread, own_lanes(mixed), ((0,), (0,))).astype(BF16)
     send_ref[...] = dot(line_ref[...], compact, ((0,), (0,))).astype(BF16).reshape(32, 16, 128)
-    spec_copy.wait()
 
 
 def pull_kernel(recv_ref, low_ref, high_ref, line_ref, spec_ref, send_ref, pair_ref):
@@ -210,7 +199,8 @@
     pair_ref[...] = jnp.concatenate(
         [spec_ref[...].reshape(16, 8, 128), compact.astype(F32).reshape(16, 8, 128)], axis=1
     ).astype(BF16)
-    rows = spread_rows(compact)
+    spread = spread_rows()
+    rows = own_lanes(dot(spread, compact))
     repeat = as_bf16((iota((128, 128), 0) & 31) == (iota((128, 128), 1) & 31))
     wide = dot(rows, repeat)
     a_real, a_imag = wide[0:256], wide[256:512]
@@ -227,7 +217,7 @@
             )
         collect = as_bf16((iota((256, 128), 0) >> 5) + t * 8 == (iota((256, 128), 1) & 31))
         pulled = pulled + dot(jnp.concatenate(parts, axis=1), collect)
-    compact = close_rows(pulled)
+    compact = dot(spread, own_lanes(pulled), ((0,), (0,))).astype(BF16)
     send_ref[...] = dot(line_ref[...], compact, ((0,), (0,))).astype(BF16).reshape(32, 16, 128)
 
 
@@ -330,12 +320,12 @@
 
 
 def weight_grad_kernel(pair_ref, out_ref):
-    row = iota((1024, 256), 0)
-    wanted = ((row >> 4) & 15) * 16 + (row >> 9) * 8 + ((row >> 8) & 1) * 4 + ((row >> 3) & 1) * 2 + (row & 1)
-    select = as_bf16(wanted == iota((1024, 256), 1))
-    rows = dot(select, pair_ref[...].reshape(256, 128))
-    row = iota((1024, 128), 0)
-    rows = jnp.where((iota((1024, 128), 1) >> 5) == ((row >> 1) & 3), rows, 0.0).astype(BF16)
+    row = iota((64, 16), 0)
+    wanted = (row >> 4) * 4 + ((row >> 3) & 1) * 2 + (row & 1)
+    select = as_bf16(wanted == iota((64, 16), 1))
+    same = (iota((64, 128), 1) >> 5) == ((iota((64, 128), 0) >> 1) & 3)
+    rows = [jnp.where(same, dot(select, pair_ref[n]), 0.0).astype(BF16) for n in range(16)]
+    rows = jnp.concatenate([rows[n][16 * k : 16 * k + 16] for k in range(4) for n in range(16)], axis=0)
     repeat = as_bf16((iota((128, 128), 0) & 31) == (iota((128, 128), 1) & 31))
     wide = dot(rows[512:1024], repeat)
     a_real, a_imag = wide[0:256], wide[256:512]
@@ -401,8 +391,7 @@
         for h in range(2)
     )
     send, spec = run(
-        mix_kernel, "mix", [piece, ((128, 128), F32)], [exchange(send, "space"), w_low, w_high, line], 10**8,
-        [pltpu.VMEM((128, 128), F32), sem], (1,),
+        mix_kernel, "mix", [piece, ((128, 128), F32)], [exchange(send, "space"), w_low, w_high, line], 10**8
     )
     bias = jnp.broadcast_to(biases[:, None], (C, 2 * NZ))
     send, delta = run(

time: 116 us -> 116 us (level)
    unnamed x16 -> x14, local copies, waits for them, and re-layouts: 3.45 us -> 3.45 us
where the time goes in v3:
time: 116 us; the launch traced here: 115 us
  blocking collectives  44.9 us (39%)
  starting transfers between devices  28.1 us (24%)
  Pallas kernels  21.3 us (18%)
  waiting for transfers between devices  16.6 us (14%)
  local copies, waits for them, and re-layouts  3.56 us (3%)
    all_to_all x3, blocking collectives, exchange(): return lax.all_to_all(value, axis, split_axis=0, concat_axis=0, tiled=True)  40.1 us
    pallas_call x8, Pallas kernels, run(): pl.pallas_call(kernel, out_shape=shapes, in_specs=[pl.BlockSpec(memory_sp...  21.3 us
    all_to_all x2, starting transfers between devices, exchange(): return lax.all_to_all(value, axis, split_axis=0, concat_axis=0, tiled=True)  17.2 us
    all_to_all x1, starting transfers between devices, body(): lax.all_to_all(copies, 'dp', 0, 0, tiled=True, axis_index_groups=same_core)  10.9 us
    all_to_all x1, waiting for transfers between devices, body(): lax.all_to_all(copies, 'dp', 0, 0, tiled=True, axis_index_groups=same_core)  9.11 us
    all_to_all x2, waiting for transfers between devices, exchange(): return lax.all_to_all(value, axis, split_axis=0, concat_axis=0, tiled=True)  7.54 us
    all_gather x2, blocking collectives, body(): lax.all_gather(blocks[4 * h:4 * h + 4], 'dp', axis=0, tiled=True, axis_in...  4.75 us
    unnamed x14, local copies, waits for them, and re-layouts  3.45 us
  transfers between devices with their start and end apart: 3, of which 3 were waited for; matrix products, arithmetic and copies ran while one was open for 0% of the time, Pallas kernels for 10%

profile of v3, /device:TPU:1, one launch (start us, length us, event | category | flops | bytes accessed | tf_op | source)
XLA Modules:
  0.0 115.2 jit_solution(16789681200336988798)
XLA Ops:
  0.6 0.0 copy-start
  0.6 0.0 copy-start.3
  0.7 1.0 copy-done.3
  1.6 0.9 repeat.1
  2.6 10.9 %all-to-all-start = ((bf16[8,16,2048]{2,1,0:T(8,128)(2,1)}), bf16[8,16,2048]{2,1,0:T(8,128)(2,1)S(1)}, u32[]{:S(2)}, u32[]{:S(2)}) async-start(bf16[8,16,2048]{2,1,0:T(8,128)(2,1)} %repeat.1), calls=%async_computation | async-start | bytes 1048576 | tf_op jit(solution)/shard_map/all_to_all | solution.py:380
  13.5 0.0 copy-start.1
  13.5 1.2 %copy-done.1 = bf16[1,32,4,32,128]{4,3,2,1,0:T(8,128)(2,1)S(1)} copy-done((bf16[1,32,4,32,128]{4,3,2,1,0:T(8,128)(2,1)S(1)}, bf16[1,32,4,32,128]{4,3,2,1,0:T(8,128)(2,1)}, u32[]{:S(2)}) %copy-start.1) | copy-done | bytes 1048600
  14.7 2.8 %regroup.1.c_hbm = bf16[256,2048]{1,0:T(8,128)(2,1)} custom-call(bf16[4096,128]{1,0:T(8,128)(2,1)S(1)} %bitcast.9), custom_call_target="tpu_custom_call" | custom-call | flops 1000000 | bytes 2097152 | tf_op jit(solution)/shard_map/regroup/pallas_call | solution.py:346
  17.5 0.0 copy-done
  17.5 0.0 copy-start.5
  17.5 1.2 %copy-done.5 = bf16[1,32,4,32,128]{4,3,2,1,0:T(8,128)(2,1)S(1)} copy-done((bf16[1,32,4,32,128]{4,3,2,1,0:T(8,128)(2,1)S(1)}, bf16[1,32,4,32,128]{4,3,2,1,0:T(8,128)(2,1)}, u32[]{:S(2)}) %copy-start.5) | copy-done | bytes 1048600
  18.7 3.6 %analyse.1 = (bf16[32,16,128]{2,1,0:T(8,128)(2,1)}, bf16[256,2048]{1,0:T(8,128)(2,1)}) custom-call(bf16[4096,128]{1,0:T(8,128)(2,1)S(1)} %bitcast.10, bf16[512,2176]{1,0:T(8,128)(2,1)S(1)} %copy-done), custom_call_target="tpu_custom_call" | custom-call | flops 1000000000 | bytes 2097152 | tf_op jit(solution)/shard_map/analyse/pallas_call | solution.py:346
  22.3 0.0 copy-start.2
  22.3 9.1 %all-to-all-done = bf16[8,16,2048]{2,1,0:T(8,128)(2,1)S(1)} async-done(((bf16[8,16,2048]{2,1,0:T(8,128)(2,1)}), bf16[8,16,2048]{2,1,0:T(8,128)(2,1)S(1)}, u32[]{:S(2)}, u32[]{:S(2)}) %all-to-all-start) | async-done | bytes 524320 | tf_op jit(solution)/shard_map/all_to_all | solution.py:380
  31.4 0.0 copy-start.6
  31.4 0.0 copy-start.4
  31.4 9.8 %all-to-all-start.1 = ((bf16[32,16,128]{2,1,0:T(8,128)(2,1)}), bf16[32,16,128]{2,1,0:T(8,128)(2,1)S(1)}, u32[]{:S(2)}, u32[]{:S(2)}) async-start(bf16[32,16,128]{2,1,0:T(8,128)(2,1)} %get-tuple-element.16), calls=%async_computation.1 | async-start | bytes 262144 | tf_op jit(solution)/shard_map/all_to_all | solution.py:363
  41.3 2.6 %all_gather.7 = bf16[8,16,2048]{2,1,0:T(8,128)(2,1)S(1)} all-gather(bf16[4,16,2048]{2,1,0:T(8,128)(2,1)S(1)} %get-tuple-element.28), channel_id=1, replica_groups={{0,32},{64,96},{128,160},{192,224},{256,288},{320,352},{384,416},{448,4..., dimensions={0}, use_global_device_ids=true | all-gather | bytes 786432 | tf_op jit(solution)/shard_map/all_gather | solution.py:390
  43.9 2.2 %all_gather.6 = bf16[8,16,2048]{2,1,0:T(8,128)(2,1)S(1)} all-gather(bf16[4,16,2048]{2,1,0:T(8,128)(2,1)S(1)} %get-tuple-element.29), channel_id=1, replica_groups={{0,32},{64,96},{128,160},{192,224},{256,288},{320,352},{384,416},{448,4..., dimensions={0}, use_global_device_ids=true | all-gather | bytes 786432 | tf_op jit(solution)/shard_map/all_gather | solution.py:390
  46.0 4.4 %all-to-all-done.1.recv_ref = bf16[32,16,128]{2,1,0:T(8,128)(2,1)S(1)} async-done(((bf16[32,16,128]{2,1,0:T(8,128)(2,1)}), bf16[32,16,128]{2,1,0:T(8,128)(2,1)S(1)}, u32[]{:S(2)}, u32[]{:S(2)}) %all-to-all-start.1) | async-done | bytes 131104 | tf_op jit(solution)/shard_map/all_to_all | solution.py:363
  50.4 0.0 copy-done.2
  50.4 1.6 %mix.1 = (bf16[32,16,128]{2,1,0:T(8,128)(2,1)S(1)}, f32[128,128]{1,0:T(8,128)S(1)}) custom-call(bf16[32,16,128]{2,1,0:T(8,128)(2,1)S(1)} %all-to-all-done.1.recv_ref, bf16[128,2048]{1,0:T(8,128)(2,1)S(1)} %bitcast.7, bf16[128,2048]{1,0:T(8,128)(2,1)S(1)} %bitcast.5, bf16[128,512]{1,0:T(8,128)(2,1)S(1)} %copy-done.2), custom_call_target="tpu_custom_call" | custom-call | flops 100000000 | bytes 2097152 | tf_op jit(solution)/shard_map/mix/pallas_call | solution.py:346
  52.1 14.1 %all_to_all.30.recv_ref = bf16[32,16,128]{2,1,0:T(8,128)(2,1)S(1)} all-to-all(bf16[32,16,128]{2,1,0:T(8,128)(2,1)S(1)} %get-tuple-element.18), channel_id=1, replica_groups=mesh['dp'=16,'space'=32] {'space'}, dimensions={0} | all-to-all | bytes 262144 | tf_op jit(solution)/shard_map/all_to_all | solution.py:363
  66.2 0.0 copy-done.6
  66.2 0.1 broadcast_in_dim.2.bias_ref
  66.2 0.0 copy-done.4
  66.2 4.5 %nonlinear.1 = (bf16[32,16,128]{2,1,0:T(8,128)(2,1)S(1)}, bf16[256,2048]{1,0:T(8,128)(2,1)}) custom-call(bf16[32,16,128]{2,1,0:T(8,128)(2,1)S(1)} %all_to_all.30.recv_ref, bf16[512,2176]{1,0:T(8,128)(2,1)S(1)} %copy-done, bf16[256,2048]{1,0:T(8,128)(2,1)} %get-tuple-element.19.x_hbm, bf16[256,2048]{1,0:T(8,128)(2,1)} %regroup.1.c_hbm, ...), custom_call_target="tpu_custom_call" | custom-call | flops 2000000000 | bytes 2097152 | tf_op jit(solution)/shard_map/nonlinear/pallas_call | solution.py:346
  70.7 13.3 %all_to_all.31.recv_ref = bf16[32,16,128]{2,1,0:T(8,128)(2,1)S(1)} all-to-all(bf16[32,16,128]{2,1,0:T(8,128)(2,1)S(1)} %get-tuple-element.21), channel_id=1, replica_groups=mesh['dp'=16,'space'=32] {'space'}, dimensions={0} | all-to-all | bytes 262144 | tf_op jit(solution)/shard_map/all_to_all | solution.py:363
  84.0 1.9 %pull.1 = (bf16[32,16,128]{2,1,0:T(8,128)(2,1)S(1)}, bf16[16,16,128]{2,1,0:T(8,128)(2,1)}) custom-call(bf16[32,16,128]{2,1,0:T(8,128)(2,1)S(1)} %all_to_all.31.recv_ref, bf16[128,2048]{1,0:T(8,128)(2,1)S(1)} %bitcast.8, bf16[128,2048]{1,0:T(8,128)(2,1)S(1)} %bitcast.6, bf16[128,512]{1,0:T(8,128)(2,1)S(1)} %copy-done.2, f32[128,128]{1,0:T(8,128)S(1)} %get-tuple-element.22.spec_ref), custom_call_target="tpu_custom_call" | custom-call | flops 100000000 | bytes 2097152 | tf_op jit(solution)/shard_map/pull/pallas_call | solution.py:346
  85.9 12.7 %all_to_all.32.recv_ref = bf16[32,16,128]{2,1,0:T(8,128)(2,1)S(1)} all-to-all(bf16[32,16,128]{2,1,0:T(8,128)(2,1)S(1)} %get-tuple-element.24), channel_id=1, replica_groups=mesh['dp'=16,'space'=32] {'space'}, dimensions={0} | all-to-all | bytes 262144 | tf_op jit(solution)/shard_map/all_to_all | solution.py:363
  98.6 7.4 %all-to-all-start.5 = ((bf16[16,16,128]{2,1,0:T(8,128)(2,1)}), bf16[16,16,128]{2,1,0:T(8,128)(2,1)S(1)}, u32[]{:S(2)}, u32[]{:S(2)}) async-start(bf16[16,16,128]{2,1,0:T(8,128)(2,1)} %get-tuple-element.27), calls=%async_computation.5 | async-start | bytes 131072 | tf_op jit(solution)/shard_map/all_to_all | solution.py:363
  105.9 4.7 %input_grad.1 = bf16[4096,128]{1,0:T(8,128)(2,1)} custom-call(bf16[32,16,128]{2,1,0:T(8,128)(2,1)S(1)} %all_to_all.32.recv_ref, bf16[512,2176]{1,0:T(8,128)(2,1)S(1)} %copy-done, bf16[256,2048]{1,0:T(8,128)(2,1)} %get-tuple-element.26.delta_hbm, bf16[32,32]{1,0:T(8,128)(2,1)S(1)} %copy-done.4), custom_call_target="tpu_custom_call" | custom-call | flops 1000000000 | bytes 2097152 | tf_op jit(solution)/shard_map/input_grad/pallas_call | solution.py:346
  110.6 3.2 %all-to-all-done.5.pair_ref = bf16[16,16,128]{2,1,0:T(8,128)(2,1)S(1)} async-done(((bf16[16,16,128]{2,1,0:T(8,128)(2,1)}), bf16[16,16,128]{2,1,0:T(8,128)(2,1)S(1)}, u32[]{:S(2)}, u32[]{:S(2)}) %all-to-all-start.5) | async-done | bytes 65568 | tf_op jit(solution)/shard_map/all_to_all | solution.py:363
  113.8 1.4 %weight_grad.1 = f32[8,2,2048]{2,1,0:T(2,128)} custom-call(bf16[16,16,128]{2,1,0:T(8,128)(2,1)S(1)} %all-to-all-done.5.pair_ref), custom_call_target="tpu_custom_call" | custom-call | flops 100000000 | bytes 2097152 | tf_op jit(solution)/shard_map/weight_grad/pallas_call | solution.py:346
  (1 shorter events, 0.0 us)
Async XLA Ops:
  0.6 16.8 %copy-start = (bf16[512,2176]{1,0:T(8,128)(2,1)S(1)}, bf16[512,2176]{1,0:T(8,128)(2,1)}, u32[]{:S(2)}) copy-start(bf16[512,2176]{1,0:T(8,128)(2,1)} %constant.4.clone.table_ref) | copy-start | bytes 6684676
  0.6 1.0 copy-start.3
  2.6 28.8 %all-to-all-start = ((bf16[8,16,2048]{2,1,0:T(8,128)(2,1)}), bf16[8,16,2048]{2,1,0:T(8,128)(2,1)S(1)}, u32[]{:S(2)}, u32[]{:S(2)}) async-start(bf16[8,16,2048]{2,1,0:T(8,128)(2,1)} %repeat.1), calls=%async_computation | async-start | bytes 1048576 | tf_op jit(solution)/shard_map/all_to_all | solution.py:380
  13.5 1.2 %copy-start.1 = (bf16[1,32,4,32,128]{4,3,2,1,0:T(8,128)(2,1)S(1)}, bf16[1,32,4,32,128]{4,3,2,1,0:T(8,128)(2,1)}, u32[]{:S(2)}) copy-start(bf16[1,32,4,32,128]{4,3,2,1,0:T(8,128)(2,1)} %param.8) | copy-start | bytes 3145732
  17.5 1.2 %copy-start.5 = (bf16[1,32,4,32,128]{4,3,2,1,0:T(8,128)(2,1)S(1)}, bf16[1,32,4,32,128]{4,3,2,1,0:T(8,128)(2,1)}, u32[]{:S(2)}) copy-start(bf16[1,32,4,32,128]{4,3,2,1,0:T(8,128)(2,1)} %param.7) | copy-start | bytes 3145732
  22.3 28.1 %copy-start.2 = (bf16[128,512]{1,0:T(8,128)(2,1)S(1)}, bf16[128,512]{1,0:T(8,128)(2,1)}, u32[]{:S(2)}) copy-start(bf16[128,512]{1,0:T(8,128)(2,1)} %constant.5.clone.line_ref) | copy-start | bytes 393220
  31.4 34.7 %copy-start.6 = (bf16[32]{0:T(256)(128)(2,1)S(1)}, bf16[32]{0:T(256)(128)(2,1)}, u32[]{:S(2)}) copy-start(bf16[32]{0:T(256)(128)(2,1)} %param.11) | copy-start | bytes 196
  31.4 34.8 %copy-start.4 = (bf16[32,32]{1,0:T(8,128)(2,1)S(1)}, bf16[32,32]{1,0:T(8,128)(2,1)}, u32[]{:S(2)}) copy-start(bf16[32,32]{1,0:T(8,128)(2,1)} %weights_ref.3) | copy-start | bytes 6148
  31.4 19.0 %all-to-all-start.1 = ((bf16[32,16,128]{2,1,0:T(8,128)(2,1)}), bf16[32,16,128]{2,1,0:T(8,128)(2,1)S(1)}, u32[]{:S(2)}, u32[]{:S(2)}) async-start(bf16[32,16,128]{2,1,0:T(8,128)(2,1)} %get-tuple-element.16), calls=%async_computation.1 | async-start | bytes 262144 | tf_op jit(solution)/shard_map/all_to_all | solution.py:363
  98.6 15.2 %all-to-all-start.5 = ((bf16[16,16,128]{2,1,0:T(8,128)(2,1)}), bf16[16,16,128]{2,1,0:T(8,128)(2,1)S(1)}, u32[]{:S(2)}, u32[]{:S(2)}) async-start(bf16[16,16,128]{2,1,0:T(8,128)(2,1)} %get-tuple-element.27), calls=%async_computation.5 | async-start | bytes 131072 | tf_op jit(solution)/shard_map/all_to_all | solution.py:363
